TPU v7x, 512 devices: a whole 4x4x16 slice. The times are simulated.
512 devices in a mesh: dp: 64 (over y_hi, z, core), seq: 8 (over x, y_lo).
Axes of the slice: x: 4, y: 4 (y_hi: 2, y_lo: 2; y = y_hi * 2 + y_lo), z: 16, core: 2. Of those that a mesh axis runs over, the one named last changes fastest.
Arguments:
- queries: bfloat16 [65536, 4096], P(('dp', 'seq')), may hold values from -180 to 180, as said below
- keys: bfloat16 [65536, 512], P(('dp', 'seq')), may hold values from -6 to 6, as said below
- values: bfloat16 [65536, 512], P(('dp', 'seq')), may hold values from -6 to 6
- lengths: int32 [64, 16], P('dp'), may hold values from 1 to 512, 1024 in all within a row
- out_grad: bfloat16 [65536, 4096], P(('dp', 'seq')), may hold values from -6 to 6
Outputs:
- attended: bfloat16 [65536, 4096], P(('dp', 'seq'))
- query_grad: bfloat16 [65536, 4096], P(('dp', 'seq'))
- key_grad: bfloat16 [65536, 512], P(('dp', 'seq'))
- value_grad: bfloat16 [65536, 512], P(('dp', 'seq'))
Inputs may be any that keep to these rules, and one draw needn't show every extreme that they name: `queries`: queries stay within this range. `keys`: keys stay within this range.
All inputs are finite; a program needn't handle non-finite values.
Results may differ from a plain program's by a relative error of at most 0.0095.
Values may be sent and summed in bfloat16 or wider, within the bound.
No kernel may reach another device: no remote copies, remote signals or barrier semaphores. Data moves between devices by JAX's collectives and lax.ppermute only.
A program may use at most 64 MiB of HBM per device.

v0:
```python
import jax
import jax.numpy as jnp
from jax import lax
from jax.sharding import PartitionSpec as P

H = 32
KVH = 4
HD = 128
GROUP = 8


def doc_of(pos, ends):
    return jnp.sum((pos[:, None] >= ends[None, :]).astype(jnp.int32), axis=1)


def shards(queries, keys, values, lengths, out_grad):
    tok_rows = queries.shape[0]
    kv_width = keys.shape[1]
    scale = HD ** (-0.5)
    qh = queries.reshape(tok_rows, KVH, GROUP, HD)
    grad_heads = out_grad.reshape(tok_rows, KVH, GROUP, HD)
    ends = jnp.cumsum(lengths[0])
    seq_pos = lax.axis_index("seq") * tok_rows + jnp.arange(tok_rows, dtype=jnp.int32)
    query_doc = doc_of(seq_pos, ends)
    total_len = tok_rows * lax.axis_size("seq")
    block = min(512, total_len)
    live_blocks = seq_pos[-1] // block + 1

    def visible_of(kstart, count):
        kpos = kstart + jnp.arange(count, dtype=jnp.int32)
        return (doc_of(kpos, ends)[None, :] == query_doc[:, None]) & (
            kpos[None, :] <= seq_pos[:, None]
        )

    def scores_of(key_rows, visible):
        raw = (
            jnp.einsum(
                "tkgd,skd->kgts",
                qh,
                key_rows.reshape(-1, KVH, HD),
                preferred_element_type=jnp.float32,
            )
            * scale
        )
        return jnp.where(visible, raw, -1e30)

    def forward_step(carry, key_rows, value_rows, kstart):
        top, lsum, acc = carry
        visible = visible_of(kstart, key_rows.shape[0])
        scores = scores_of(key_rows, visible)
        top_new = jnp.maximum(top, jnp.max(scores, axis=-1))
        rescale = jnp.exp(top - top_new)
        expo = jnp.where(visible, jnp.exp(scores - top_new[..., None]), 0.0)
        lsum = lsum * rescale + jnp.sum(expo, axis=-1)
        acc = acc * rescale[..., None] + jnp.einsum(
            "kgts,skd->kgtd",
            expo.astype(jnp.bfloat16),
            value_rows.reshape(-1, KVH, HD),
            preferred_element_type=jnp.float32,
        )
        return (top_new, lsum, acc)

    start_carry = (
        jnp.full((KVH, GROUP, tok_rows), -1e30, jnp.float32),
        jnp.zeros((KVH, GROUP, tok_rows), jnp.float32),
        jnp.zeros((KVH, GROUP, tok_rows, HD), jnp.float32),
    )
    key_all, value_all = (
        lax.all_gather(keys, "seq", axis=0, tiled=True),
        lax.all_gather(values, "seq", axis=0, tiled=True),
    )

    def forward_block(index, carry):
        kstart = index * block
        key_rows = lax.dynamic_slice_in_dim(key_all, kstart, block, 0)
        value_rows = lax.dynamic_slice_in_dim(value_all, kstart, block, 0)
        return forward_step(carry, key_rows, value_rows, kstart)

    top, lsum, acc = lax.fori_loop(0, live_blocks, forward_block, start_carry)
    heads_out = acc / lsum[..., None]
    attended = heads_out.transpose(2, 0, 1, 3).reshape(tok_rows, H * HD).astype(jnp.bfloat16)
    rowdot = jnp.sum(
        out_grad.astype(jnp.float32).reshape(tok_rows, KVH, GROUP, HD)
        * attended.astype(jnp.float32).reshape(tok_rows, KVH, GROUP, HD),
        axis=-1,
    ).transpose(1, 2, 0)

    def backward_block(index, carry):
        query_acc, partial_value = carry
        kstart = index * block
        key_rows = lax.dynamic_slice_in_dim(key_all, kstart, block, 0)
        value_rows = lax.dynamic_slice_in_dim(value_all, kstart, block, 0)
        visible = visible_of(kstart, block)
        scores = scores_of(key_rows, visible)
        probs = jnp.where(visible, jnp.exp(scores - top[..., None]) / lsum[..., None], 0.0)
        value_heads = value_rows.reshape(block, KVH, HD)
        key_heads = key_rows.reshape(block, KVH, HD)
        dprobs = jnp.einsum(
            "tkgd,skd->kgts", grad_heads, value_heads, preferred_element_type=jnp.float32
        )
        dscores = (probs * (dprobs - rowdot[..., None])).astype(jnp.bfloat16)
        query_acc = query_acc + jnp.einsum(
            "kgts,skd->kgtd", dscores, key_heads, preferred_element_type=jnp.float32
        )
        key_part = (
            jnp.einsum("kgts,tkgd->skd", dscores, qh, preferred_element_type=jnp.float32) * scale
        )
        value_part = jnp.einsum(
            "kgts,tkgd->skd",
            probs.astype(jnp.bfloat16),
            grad_heads,
            preferred_element_type=jnp.float32,
        )
        stacked = jnp.concatenate(
            [key_part.reshape(block, kv_width), value_part.reshape(block, kv_width)], axis=1
        )
        partial_value = lax.dynamic_update_slice(
            partial_value, stacked.astype(jnp.bfloat16), (kstart, 0)
        )
        return (query_acc, partial_value)

    back_carry = (
        jnp.zeros((KVH, GROUP, tok_rows, HD), jnp.float32),
        jnp.zeros((total_len, 2 * kv_width), jnp.bfloat16),
    )
    query_acc, partial_value = lax.fori_loop(0, live_blocks, backward_block, back_carry)
    summed = lax.psum_scatter(partial_value, "seq", scatter_dimension=0, tiled=True).astype(
        jnp.float32
    )
    query_grad = (
        (query_acc * scale).transpose(2, 0, 1, 3).reshape(tok_rows, H * HD).astype(jnp.bfloat16)
    )
    key_grad = summed[:, :kv_width].astype(jnp.bfloat16)
    value_grad = summed[:, kv_width:].astype(jnp.bfloat16)
    return (attended, query_grad, key_grad, value_grad)


def solution(mesh):
    in_specs = (
        P(("dp", "seq"), None),
        P(("dp", "seq"), None),
        P(("dp", "seq"), None),
        P("dp", None),
        P(("dp", "seq"), None),
    )
    out_specs = (
        P(("dp", "seq"), None),
        P(("dp", "seq"), None),
        P(("dp", "seq"), None),
        P(("dp", "seq"), None),
    )
    return jax.shard_map(shards, mesh=mesh, in_specs=in_specs, out_specs=out_specs, check_vma=False)
```

profile of v0, /device:TPU:42, one launch (start us, length us, event | category | flops | bytes accessed | tf_op | source)
XLA Modules:
  0.0 249.3 jit_solution(3896361902892705112)
XLA Ops:
  7.2 0.0 all-gather.3.cloned.1.call-start
  7.2 1.7 copy.56
  8.9 0.0 all-gather.3.cloned.1.call-update
  8.9 0.0 all-gather.5.cloned.1.call-start
  8.9 1.7 copy.58
  10.6 0.0 all-gather.5.cloned.1.call-update
  10.6 0.0 reduce-scatter.2.cloned.1.call-start
  10.7 0.6 slice.11
  13.9 0.7 copy.55
  14.7 0.1 reduce
  14.8 1.6 copy.62
  16.4 2.3 copy.57
  18.7 1.6 copy.59
  20.3 0.1 convert_reduce_fusion.2
  20.4 42.1 %all-gather.3.cloned.1.call-done = bf16[1024,512]{0,1:T(8,128)(2,1)} async-done(((bf16[128,512]{0,1:T(8,128)(2,1)}), bf16[1024,512]{0,1:T(8,128)(2,1)}) %all-gather.3.cloned.1.call-update) | async-done | bytes 1048592 | tf_op jit(solution)/shard_map/all_gather | solution.py:69
  62.5 53.0 %all-gather.5.cloned.1.call-done = bf16[1024,512]{0,1:T(8,128)(2,1)} async-done(((bf16[128,512]{0,1:T(8,128)(2,1)}), bf16[1024,512]{0,1:T(8,128)(2,1)}) %all-gather.5.cloned.1.call-update) | async-done | bytes 1048592 | tf_op jit(solution)/shard_map/all_gather | solution.py:70
  115.5 1.6 broadcast.53.clone
  117.1 10.0 %while.28 = (s32[]{:T(128)}, f32[4,8,128]{2,1,0:T(8,128)S(1)}, f32[4,8,128]{2,1,0:T(8,128)S(1)}, f32[4,8,128,128]{3,2,1,0:T(8,128)}, s32[]{:T(128)}, /*index=5*/...) while((s32[]{:T(128)}, f32[4,8,128]{2,1,0:T(8,128)S(1)}, ...), condition=%wide.region_6.7_spmd.clone, body=%wide.region_2.6_spmd.clone.sunk | while | flops 1102282880 | bytes 50868028 | solution.py:79
  117.1 0.1 convert_reduce_fusion.5
  117.2 0.2 compare_and_fusion.4
  117.4 1.3 constant_dynamic-slice_fusion.6
  118.7 1.5 fusion.69
  120.2 2.1 fusion.70
  122.3 3.4 %multiply_add_fusion.5 = f32[4,8,128,128]{3,2,1,0:T(8,128)S(1)} fusion(f32[4,8,128,128]{3,2,1,0:T(8,128)S(1)} %copy-done, bf16[512,4,128,1]{0,2,3,1:T(8,128)(2,1)S(1)} %bitcast.153, f32[4,512,128,8]{2,1,3,0:T(8,128)S(1)} %get-tuple-element.446, f32[4,8,128]{2,1,0:T(8,128)S(1)} %max.5, pred[128,512]{0,1:T(8,128)(4,1)S(1)} %compare_and_fusion.4, ...), kind=kOutput, calls=%fused_computation.9.clone.1 | convolution fusion | flops 548405248 | bytes 13205504 | tf_op jit(solution)/shard_map/while/body/kgts,skd->kgtd/dot_general | solution.py:55
  125.7 1.3 copy-done.1
  127.1 1.9 copy.60
  129.0 1.5 multiply_reduce_fusion
  130.5 1.6 broadcast.53
  132.1 1.6 broadcast_in_dim.53.clone
  133.7 17.2 %while.29 = (s32[]{:T(128)}, f32[4,8,128,128]{3,2,1,0:T(8,128)}, bf16[1024,1024]{1,0:T(8,128)(2,1)}, s32[]{:T(128)}, s32[16]{0:T(128)S(1)}, /*index=5*/s32[128]{...) while((s32[]{:T(128)}, f32[4,8,128,128]{3,2,1,0:T(8,128)}, ...), condition=%wide.region_10.11_spmd.clone, body=%wide.region_8.10_spmd.clone.sunk | while | flops 2706857984 | bytes 57339684 | solution.py:126
  133.7 0.1 convert_reduce_fusion.6
  133.8 0.2 compare_and_fusion.5
  134.0 1.3 constant_dynamic-slice_fusion.7
  135.3 3.8 %fusion.81 = f32[4,8,128,512]{2,3,1,0:T(8,128)S(1)} fusion(f32[4,8,128]{2,1,0:T(8,128)S(1)} %get-tuple-element.556, f32[4,8,128]{2,1,0:T(8,128)S(1)} %get-tuple-element.555, pred[128,512]{0,1:T(8,128)(4,1)S(1)} %compare_and_fusion.5, bf16[512,4,128,1]{0,2,3,1:T(8,128)(2,1)S(1)} %bitcast.149, bf16[128,4,8,128]{0,3,2,1:T(8,128)(2,1)} %get-tuple-element.554), kind=kOutput, calls=%fused_computation.28.clone.1 | convolution fusion | flops 547356672 | bytes 10059776 | tf_op jit(solution)/shard_map/while/body/tkgd,skd->kgts/dot_general | solution.py:37
  139.1 1.5 fusion.83
  140.6 1.4 fusion.82
  142.0 2.7 %fusion.84 = bf16[4,512,128]{1,2,0:T(8,128)(2,1)S(1)} fusion(bf16[4,8,128,512]{2,3,1,0:T(8,128)(2,1)S(1)} %fusion.82, bf16[128,4,8,128]{0,3,2,1:T(8,128)(2,1)} %get-tuple-element.554), kind=kOutput, calls=%fused_computation.36.clone.1 | convolution fusion | flops 537395200 | bytes 5767168 | tf_op jit(solution)/shard_map/while/body/kgts,tkgd->skd/dot_general | solution.py:106
  144.7 4.5 %convolution_add_fusion.2 = f32[4,8,128,128]{3,2,1,0:T(8,128)} fusion(f32[4,8,128,128]{3,2,1,0:T(8,128)} %get-tuple-element.530, bf16[4,8,128,512]{2,3,1,0:T(8,128)(2,1)S(1)} %fusion.82, bf16[512,4,128,1]{0,2,3,1:T(8,128)(2,1)S(1)} %bitcast.150), kind=kOutput, calls=%fused_computation.31.clone.1 | convolution fusion | flops 537395200 | bytes 8912896 | tf_op jit(solution)/shard_map/while/body/kgts,skd->kgtd/dot_general | solution.py:102
  149.2 0.1 pad_maximum_fusion.2
  149.3 0.5 copy.95
  149.9 1.1 constant_dynamic-update-slice_fusion.2
  150.9 0.0 reduce-scatter.2.cloned.1.call-update
  150.9 2.3 copy.78
  153.2 1.9 fusion.31
  155.1 0.7 copy.63
  155.8 1.4 copy.93
  157.2 83.9 %reduce-scatter.2.cloned.1.call-done = bf16[128,1024]{1,0:T(8,128)(2,1)} async-done(((bf16[1024,1024]{1,0:T(8,128)(2,1)}), bf16[128,1024]{1,0:T(8,128)(2,1)}) %reduce-scatter.2.cloned.1.call-update) | async-done | bytes 262160 | tf_op jit(solution)/shard_map/reduce_scatter | solution.py:127
  241.1 1.7 fusion.32
  (14 shorter events, 0.1 us)
Async XLA Ops:
  7.2 55.3 %all-gather.3.cloned.1.call-start = ((), (), s32[]{:S(2)}) async-start(), calls=%async_computation.1 | async-start | bytes 1179648 | tf_op jit(solution)/shard_map/all_gather | solution.py:69
  8.9 106.6 %all-gather.5.cloned.1.call-start = ((), (), s32[]{:S(2)}) async-start(), calls=%async_computation.2 | async-start | bytes 1179648 | tf_op jit(solution)/shard_map/all_gather | solution.py:70
  10.6 230.4 %reduce-scatter.2.cloned.1.call-start = ((), (), s32[]{:S(2)}) async-start(), calls=%async_computation.3 | async-start | bytes 2359296 | tf_op jit(solution)/shard_map/reduce_scatter | solution.py:127
  120.1 2.2 copy-start
  125.7 1.4 copy-start.1
Sparse Core Ops, SparseCore 0:
  10.6 51.9 all-gather.2
  65.1 50.3 all-gather.4
  151.1 89.9 reduce-scatter.1
where the time goes:
time: 250 us; the launch traced here: 249 us
  waiting for transfers between devices  179 us (72%)
  local copies, waits for them, and re-layouts  28.3 us (11%)
  matrix products  18.8 us (8%)
  between operations  16.4 us (7%)
  other arithmetic  6.46 us (3%)
    reduce_scatter x1, waiting for transfers between devices, shards(): lax.psum_scatter(partial_value, 'seq', scatter_dimension=0, tiled=True)  83.9 us
    all_gather x1, waiting for transfers between devices, shards(): lax.all_gather(values, 'seq', axis=0, tiled=True)  53 us
    all_gather x1, waiting for transfers between devices, shards(): lax.all_gather(keys, 'seq', axis=0, tiled=True)  42.1 us
    unnamed x6, local copies, waits for them, and re-layouts  10.2 us
    dot_general x2, matrix products, scores_of(): jnp.einsum('tkgd,skd->kgts', qh, key_rows.reshape(-1, KVH, HD), preferred...  5.27 us
  transfers between devices with their start and end apart: 3, of which 3 were waited for; matrix products, arithmetic and copies ran while one was open for 6% of the time, Pallas kernels for 0%

commit v1 on v0

v1 whole, which is shorter than its diff:
```python
import functools

import jax
import jax.numpy as jnp
from jax import lax
from jax.experimental import pallas as pl
from jax.experimental.pallas import tpu as pltpu
from jax.sharding import PartitionSpec as P

H = 32
KVH = 4
HD = 128
GROUP = 8
SEGS = 16
MOST = 512
SCALE = HD**-0.5
EXP2_SCALE = SCALE * 1.4426950408889634
NEG = -1e30
ROWS = 128
HEADS_AT_ONCE = 4

NT = (((1,), (1,)), ((), ()))
TN = (((0,), (0,)), ((), ()))


def dot(a, b, dims=(((1,), (0,)), ((), ()))):
    return lax.dot_general(a, b, dims, preferred_element_type=jnp.float32)


def attend(chunks, lens_ref, where_ref, q_ref, g_ref, *refs):
    k_refs, v_refs = refs[:chunks], refs[chunks : 2 * chunks]
    att_ref, dq_ref = refs[2 * chunks : 2 * chunks + 2]
    part_refs = refs[2 * chunks + 2 : 3 * chunks + 2]
    bias_ref, dk_ref, dv_ref = refs[3 * chunks + 2 :]
    keys_n = chunks * ROWS

    @pl.when(pl.program_id(0) == 0)
    def _():
        run = where_ref[0]
        pos = run * ROWS + lax.broadcasted_iota(jnp.int32, (ROWS, ROWS), 0)
        lane = lax.broadcasted_iota(jnp.int32, (ROWS, ROWS), 1)
        start = jnp.zeros((ROWS, ROWS), jnp.int32)
        end = jnp.int32(0)
        for d in range(SEGS):
            end = end + lens_ref[d]
            start = jnp.where(pos >= end, end, start)
        for c in range(chunks):
            key_pos = (run - c) * ROWS + lane
            seen = (key_pos >= start) & (key_pos <= pos)
            bias_ref[:, c * ROWS : (c + 1) * ROWS] = jnp.where(seen, 0.0, NEG)

    k = jnp.concatenate([r[...] for r in k_refs], axis=0)
    v = jnp.concatenate([r[...] for r in v_refs], axis=0)
    ones = jnp.ones((keys_n, HD), jnp.bfloat16)
    v_one = jnp.concatenate([v, ones], axis=1)
    bias = bias_ref[...]
    many = HEADS_AT_ONCE
    for first in range(0, GROUP, many):
        heads = [slice(h * HD, (h + 1) * HD) for h in range(first, first + many)]
        q = jnp.concatenate([q_ref[:, h] for h in heads], axis=0)
        g = jnp.concatenate([g_ref[:, h] for h in heads], axis=0).astype(jnp.float32)
        scores = dot(q, k, NT) + jnp.concatenate([bias] * many, axis=0)
        top = jnp.max(scores, axis=1, keepdims=True)
        expo = jnp.exp2((scores - top) * EXP2_SCALE)
        weights = expo.astype(jnp.bfloat16)
        out = dot(weights, v_one)
        inv = 1.0 / out[:, HD:]
        att = (out[:, :HD] * inv).astype(jnp.bfloat16)
        rowdot = jnp.sum(g * att.astype(jnp.float32) * inv, axis=1, keepdims=True)
        g_scaled = (g * inv).astype(jnp.bfloat16)
        dprobs = dot(g_scaled, v, NT)
        dscores = (expo * (dprobs - rowdot)).astype(jnp.bfloat16)
        dq = (dot(dscores, k) * SCALE).astype(jnp.bfloat16)
        for i, h in enumerate(heads):
            att_ref[:, h] = att[i * ROWS : (i + 1) * ROWS]
            dq_ref[:, h] = dq[i * ROWS : (i + 1) * ROWS]
        dk, dv = dot(q, dscores, TN), dot(g_scaled, weights, TN)
        if first == 0:
            dk_ref[...], dv_ref[...] = dk, dv
        else:
            dk_ref[...] += dk
            dv_ref[...] += dv
    for c in range(chunks):
        cols = slice(c * ROWS, (c + 1) * ROWS)
        part_refs[c][0, 0] = (dk_ref[:, cols] * SCALE).astype(jnp.bfloat16)
        part_refs[c][0, 1] = dv_ref[:, cols].astype(jnp.bfloat16)


def total(*refs):
    part_refs, (dk_ref, dv_ref) = refs[:-2], refs[-2:]
    for h in range(KVH):
        for i, o_ref in enumerate((dk_ref, dv_ref)):
            s = part_refs[0][h, i].astype(jnp.float32)
            for r in part_refs[1:]:
                s = s + r[h, i].astype(jnp.float32)
            o_ref[:, h * HD : (h + 1) * HD] = s.T.astype(jnp.bfloat16)


def shards(queries, keys, values, lengths, out_grad):
    n = lax.axis_size("seq")
    back = min(n - 1, -(-(MOST - 1) // ROWS))
    chunks = back + 1
    run = lax.axis_index("seq").astype(jnp.int32)
    both = jnp.concatenate([keys, values], axis=1)
    got = [
        lax.ppermute(both, "seq", [(i, i + c) for i in range(n - c)])
        for c in range(1, chunks)
    ]
    wide = pl.BlockSpec((ROWS, GROUP * HD), lambda h, *_: (0, h))
    k_spec = pl.BlockSpec((ROWS, HD), lambda h, *_: (0, h))
    v_spec = pl.BlockSpec((ROWS, HD), lambda h, *_: (0, KVH + h))
    part = pl.BlockSpec((1, 2, HD, ROWS), lambda h, *_: (h, 0, 0, 0))
    part_shape = jax.ShapeDtypeStruct((KVH, 2, HD, ROWS), jnp.bfloat16)
    big = jax.ShapeDtypeStruct((ROWS, H * HD), jnp.bfloat16)
    att, dq, *parts = pl.pallas_call(
        functools.partial(attend, chunks),
        grid_spec=pltpu.PrefetchScalarGridSpec(
            num_scalar_prefetch=2,
            grid=(KVH,),
            in_specs=[wide, wide]
            + [k_spec] * chunks
            + [k_spec]
            + [v_spec] * back,
            out_specs=[wide, wide] + [part] * chunks,
            scratch_shapes=[
                pltpu.VMEM((ROWS, chunks * ROWS), jnp.float32),
                pltpu.VMEM((HD, chunks * ROWS), jnp.float32),
                pltpu.VMEM((HD, chunks * ROWS), jnp.float32),
            ],
        ),
        out_shape=[big, big] + [part_shape] * chunks,
        name="attend",
    )(lengths[0], run[None], queries, out_grad, keys, *got, values, *got)
    sent = [
        lax.ppermute(parts[c], "seq", [(i, i - c) for i in range(c, n)])
        for c in range(1, chunks)
    ]
    small = jax.ShapeDtypeStruct((ROWS, KVH * HD), jnp.bfloat16)
    dk, dv = pl.pallas_call(total, out_shape=[small, small], name="total")(
        parts[0], *sent
    )
    return att, dq, dk, dv


def solution(mesh):
    rows = P(("dp", "seq"), None)
    return jax.shard_map(
        shards,
        mesh=mesh,
        in_specs=(rows, rows, rows, P("dp", None), rows),
        out_specs=(rows,) * 4,
        check_vma=False,
    )
```

time: 250 us -> 77.7 us (0.31)
  the two profiles are of different devices: /device:TPU:42 before, /device:TPU:450 now
where the time goes in v1:
time: 77.7 us; the launch traced here: 77.4 us
  waiting for transfers between devices  38.4 us (49%)
  Pallas kernels  17.9 us (23%)
  starting transfers between devices  17.8 us (23%)
  local copies, waits for them, and re-layouts  2.56 us (3%)
    ppermute x4, waiting for transfers between devices, shards(): lax.ppermute(parts[c], 'seq', [(i, i - c) for i in range(c, n)])  20.4 us
    ppermute x4, waiting for transfers between devices, shards(): lax.ppermute(both, 'seq', [(i, i + c) for i in range(n - c)])  18 us
    pallas_call x1, Pallas kernels, shards(): pl.pallas_call(functools.partial(attend, chunks), grid_spec=pltpu.Prefetc...  15.7 us
    ppermute x4, starting transfers between devices, shards(): lax.ppermute(both, 'seq', [(i, i + c) for i in range(n - c)])  11.4 us
    ppermute x4, starting transfers between devices, shards(): lax.ppermute(parts[c], 'seq', [(i, i - c) for i in range(c, n)])  6.42 us
    unnamed x19, local copies, waits for them, and re-layouts  2.55 us
    pallas_call x1, Pallas kernels, shards(): pl.pallas_call(total, out_shape=[small, small], name='total')  2.2 us
  transfers between devices with their start and end apart: 8, of which 5 were waited for; matrix products, arithmetic and copies ran while one was open for 0% of the time, Pallas kernels for 0%

profile of v1, /device:TPU:450, one launch (start us, length us, event | category | flops | bytes accessed | tf_op | source)
XLA Modules:
  0.0 77.4 jit_solution(7533335352813790121)
XLA Ops:
  0.6 0.0 copy-start.4
  0.6 1.0 %constant_dynamic-update-slice_fusion.1 = bf16[128,1024]{1,0:T(8,128)(2,1)S(1)} fusion(bf16[128,512]{1,0:T(8,128)(2,1)} %refs_0_.1), kind=kLoop, calls=%fused_computation.1 | loop fusion | bytes 262144
  1.6 0.0 copy-done.4
  1.6 4.0 %collective-permute-start.3 = (bf16[128,1024]{1,0:T(8,128)(2,1)S(1)}, bf16[128,1024]{1,0:T(8,128)(2,1)S(1)}, u32[]{:S(2)}, u32[]{:S(2)}) collective-permute-start(bf16[128,1024]{1,0:T(8,128)(2,1)S(1)} %constant_dynamic-update-slice_fusion), channel_id=1, source_target_pairs={{0,4},{1,5},{2,6},{3,7},{8,12},{9,13},{10,14},{11,15},{16,20},{17,... | collective-permute-start | bytes 786440 | tf_op jit(solution)/shard_map/ppermute | solution.py:106
  5.7 1.7 %collective-permute-start.2 = (bf16[128,1024]{1,0:T(8,128)(2,1)S(1)}, bf16[128,1024]{1,0:T(8,128)(2,1)S(1)}, u32[]{:S(2)}, u32[]{:S(2)}) collective-permute-start(bf16[128,1024]{1,0:T(8,128)(2,1)S(1)} %constant_dynamic-update-slice_fusion), channel_id=1, source_target_pairs={{0,3},{1,4},{2,5},{3,6},{4,7},{8,11},{9,12},{10,13},{11,14},{12,15... | collective-permute-start | bytes 786440 | tf_op jit(solution)/shard_map/ppermute | solution.py:106
  7.4 3.1 %collective-permute-start.1 = (bf16[128,1024]{1,0:T(8,128)(2,1)S(1)}, bf16[128,1024]{1,0:T(8,128)(2,1)S(1)}, u32[]{:S(2)}, u32[]{:S(2)}) collective-permute-start(bf16[128,1024]{1,0:T(8,128)(2,1)S(1)} %constant_dynamic-update-slice_fusion), channel_id=1, source_target_pairs={{0,2},{1,3},{2,4},{3,5},{4,6},{5,7},{8,10},{9,11},{10,12},{11,13},... | collective-permute-start | bytes 786440 | tf_op jit(solution)/shard_map/ppermute | solution.py:106
  10.5 2.6 %collective-permute-start = (bf16[128,1024]{1,0:T(8,128)(2,1)S(1)}, bf16[128,1024]{1,0:T(8,128)(2,1)S(1)}, u32[]{:S(2)}, u32[]{:S(2)}) collective-permute-start(bf16[128,1024]{1,0:T(8,128)(2,1)S(1)} %constant_dynamic-update-slice_fusion), channel_id=1, source_target_pairs={{0,1},{1,2},{2,3},{3,4},{4,5},{5,6},{6,7},{8,9},{9,10},{10,11},{11... | collective-permute-start | bytes 786440 | tf_op jit(solution)/shard_map/ppermute | solution.py:106
  13.0 0.0 collective-permute-done.3.refs_4_.refs_9_
  13.0 0.0 copy-start
  13.1 4.8 %collective-permute-done.2.refs_3_.refs_8_ = bf16[128,1024]{1,0:T(8,128)(2,1)S(1)} collective-permute-done((bf16[128,1024]{1,0:T(8,128)(2,1)S(1)}, bf16[128,1024]{1,0:T(8,128)(2,1)S(1)}, u32[]{:S(2)}, u32[]{:S(2)}) %collective-permute-start.2) | collective-permute-done | bytes 262176 | tf_op jit(solution)/shard_map/ppermute | solution.py:106
  17.8 0.0 copy-start.1
  17.8 6.6 %collective-permute-done.1.refs_2_.refs_7_ = bf16[128,1024]{1,0:T(8,128)(2,1)S(1)} collective-permute-done((bf16[128,1024]{1,0:T(8,128)(2,1)S(1)}, bf16[128,1024]{1,0:T(8,128)(2,1)S(1)}, u32[]{:S(2)}, u32[]{:S(2)}) %collective-permute-start.1) | collective-permute-done | bytes 262176 | tf_op jit(solution)/shard_map/ppermute | solution.py:106
  24.4 0.0 copy-start.2
  24.4 6.6 %collective-permute-done.refs_1_.refs_6_ = bf16[128,1024]{1,0:T(8,128)(2,1)S(1)} collective-permute-done((bf16[128,1024]{1,0:T(8,128)(2,1)S(1)}, bf16[128,1024]{1,0:T(8,128)(2,1)S(1)}, u32[]{:S(2)}, u32[]{:S(2)}) %collective-permute-start) | collective-permute-done | bytes 262176 | tf_op jit(solution)/shard_map/ppermute | solution.py:106
  31.0 0.0 copy-start.3
  31.0 0.0 copy-done
  31.0 0.0 copy-done.1
  31.0 0.0 copy-done.2
  31.0 0.7 copy-done.3
  31.7 15.7 %attend.1 = (bf16[128,4096]{1,0:T(8,128)(2,1)}, bf16[128,4096]{1,0:T(8,128)(2,1)}, bf16[4,2,128,128]{3,2,1,0:T(8,128)(2,1)}, bf16[4,2,128,128]{3,2,1,0:T(8,128)(...) custom-call(s32[16]{0:T(128)} %bitcast.2, ...), custom_call_target="tpu_custom_call" | custom-call | tf_op jit(solution)/shard_map/attend/pallas_call | solution.py:115
  47.4 1.9 %collective-permute-start.4 = (bf16[4,2,128,128]{3,2,1,0:T(8,128)(2,1)}, bf16[4,2,128,128]{3,2,1,0:T(8,128)(2,1)S(1)}, u32[]{:S(2)}, u32[]{:S(2)}) collective-permute-start(bf16[4,2,128,128]{3,2,1,0:T(8,128)(2,1)} %get-tuple-element.16), channel_id=1, source_target_pairs={{1,0},{2,1},{3,2},{4,3},{5,4},{6,5},{7,6},{9,8},{10,9},{11,10},{12... | collective-permute-start | bytes 786440 | tf_op jit(solution)/shard_map/ppermute | solution.py:135
  49.3 1.9 %collective-permute-start.5 = (bf16[4,2,128,128]{3,2,1,0:T(8,128)(2,1)}, bf16[4,2,128,128]{3,2,1,0:T(8,128)(2,1)S(1)}, u32[]{:S(2)}, u32[]{:S(2)}) collective-permute-start(bf16[4,2,128,128]{3,2,1,0:T(8,128)(2,1)} %get-tuple-element.17), channel_id=1, source_target_pairs={{2,0},{3,1},{4,2},{5,3},{6,4},{7,5},{10,8},{11,9},{12,10},{13,11},... | collective-permute-start | bytes 786440 | tf_op jit(solution)/shard_map/ppermute | solution.py:135
  51.2 1.3 %collective-permute-start.6 = (bf16[4,2,128,128]{3,2,1,0:T(8,128)(2,1)}, bf16[4,2,128,128]{3,2,1,0:T(8,128)(2,1)S(1)}, u32[]{:S(2)}, u32[]{:S(2)}) collective-permute-start(bf16[4,2,128,128]{3,2,1,0:T(8,128)(2,1)} %get-tuple-element.18), channel_id=1, source_target_pairs={{3,0},{4,1},{5,2},{6,3},{7,4},{11,8},{12,9},{13,10},{14,11},{15,12... | collective-permute-start | bytes 786440 | tf_op jit(solution)/shard_map/ppermute | solution.py:135
  52.5 1.3 %collective-permute-start.7 = (bf16[4,2,128,128]{3,2,1,0:T(8,128)(2,1)}, bf16[4,2,128,128]{3,2,1,0:T(8,128)(2,1)S(1)}, u32[]{:S(2)}, u32[]{:S(2)}) collective-permute-start(bf16[4,2,128,128]{3,2,1,0:T(8,128)(2,1)} %get-tuple-element.19), channel_id=1, source_target_pairs={{4,0},{5,1},{6,2},{7,3},{12,8},{13,9},{14,10},{15,11},{20,16},{21,... | collective-permute-start | bytes 786440 | tf_op jit(solution)/shard_map/ppermute | solution.py:135
  53.8 2.8 %collective-permute-done.4.refs_1_ = bf16[4,2,128,128]{3,2,1,0:T(8,128)(2,1)S(1)} collective-permute-done((bf16[4,2,128,128]{3,2,1,0:T(8,128)(2,1)}, bf16[4,2,128,128]{3,2,1,0:T(8,128)(2,1)S(1)}, u32[]{:S(2)}, u32[]{:S(2)}) %collective-permute-start.4) | collective-permute-done | bytes 262176 | tf_op jit(solution)/shard_map/ppermute | solution.py:135
  56.7 0.0 copy-start.5
  56.7 17.6 %collective-permute-done.5.refs_2_ = bf16[4,2,128,128]{3,2,1,0:T(8,128)(2,1)S(1)} collective-permute-done((bf16[4,2,128,128]{3,2,1,0:T(8,128)(2,1)}, bf16[4,2,128,128]{3,2,1,0:T(8,128)(2,1)S(1)}, u32[]{:S(2)}, u32[]{:S(2)}) %collective-permute-start.5) | collective-permute-done | bytes 262176 | tf_op jit(solution)/shard_map/ppermute | solution.py:135
  74.3 0.0 copy-start.6
  74.3 0.0 collective-permute-done.6.refs_3_
  74.3 0.0 copy-start.7
  74.3 0.0 collective-permute-done.7.refs_4_
  74.3 0.0 copy-start.8
  74.3 0.0 copy-done.5
  74.3 0.7 copy-done.6
  75.0 0.1 copy-done.7
  75.1 0.1 copy-done.8
  75.2 2.2 %total.1 = (bf16[128,512]{1,0:T(8,128)(2,1)}, bf16[128,512]{1,0:T(8,128)(2,1)}) custom-call(bf16[4,2,128,128]{3,2,1,0:T(8,128)(2,1)} %get-tuple-element.15.refs_0_, bf16[4,2,128,128]{3,2,1,0:T(8,128)(2,1)} %copy-done.5, bf16[4,2,128,128]{3,2,1,0:T(8,128)(2,1)} %copy-done.6, bf16[4,2,128,128]{3,2,1,0:T(8,128)(2,1)} %copy-done.7, ...), custom_call_target="tpu_custom_call" | custom-call | tf_op jit(solution)/shard_map/total/pallas_call | solution.py:139
  (1 shorter events, 0.0 us)
Async XLA Ops:
  0.6 1.0 %copy-start.4 = (bf16[128,512]{1,0:T(8,128)(2,1)S(1)}, bf16[128,512]{1,0:T(8,128)(2,1)}, u32[]{:S(2)}) copy-start(bf16[128,512]{1,0:T(8,128)(2,1)} %refs_5_.1) | copy-start | bytes 393220
  1.6 11.4 %collective-permute-start.3 = (bf16[128,1024]{1,0:T(8,128)(2,1)S(1)}, bf16[128,1024]{1,0:T(8,128)(2,1)S(1)}, u32[]{:S(2)}, u32[]{:S(2)}) collective-permute-start(bf16[128,1024]{1,0:T(8,128)(2,1)S(1)} %constant_dynamic-update-slice_fusion), channel_id=1, source_target_pairs={{0,4},{1,5},{2,6},{3,7},{8,12},{9,13},{10,14},{11,15},{16,20},{17,... | collective-permute-start | bytes 786440 | tf_op jit(solution)/shard_map/ppermute | solution.py:106
  5.7 12.2 %collective-permute-start.2 = (bf16[128,1024]{1,0:T(8,128)(2,1)S(1)}, bf16[128,1024]{1,0:T(8,128)(2,1)S(1)}, u32[]{:S(2)}, u32[]{:S(2)}) collective-permute-start(bf16[128,1024]{1,0:T(8,128)(2,1)S(1)} %constant_dynamic-update-slice_fusion), channel_id=1, source_target_pairs={{0,3},{1,4},{2,5},{3,6},{4,7},{8,11},{9,12},{10,13},{11,14},{12,15... | collective-permute-start | bytes 786440 | tf_op jit(solution)/shard_map/ppermute | solution.py:106
  7.4 17.1 %collective-permute-start.1 = (bf16[128,1024]{1,0:T(8,128)(2,1)S(1)}, bf16[128,1024]{1,0:T(8,128)(2,1)S(1)}, u32[]{:S(2)}, u32[]{:S(2)}) collective-permute-start(bf16[128,1024]{1,0:T(8,128)(2,1)S(1)} %constant_dynamic-update-slice_fusion), channel_id=1, source_target_pairs={{0,2},{1,3},{2,4},{3,5},{4,6},{5,7},{8,10},{9,11},{10,12},{11,13},... | collective-permute-start | bytes 786440 | tf_op jit(solution)/shard_map/ppermute | solution.py:106
  10.5 20.5 %collective-permute-start = (bf16[128,1024]{1,0:T(8,128)(2,1)S(1)}, bf16[128,1024]{1,0:T(8,128)(2,1)S(1)}, u32[]{:S(2)}, u32[]{:S(2)}) collective-permute-start(bf16[128,1024]{1,0:T(8,128)(2,1)S(1)} %constant_dynamic-update-slice_fusion), channel_id=1, source_target_pairs={{0,1},{1,2},{2,3},{3,4},{4,5},{5,6},{6,7},{8,9},{9,10},{10,11},{11... | collective-permute-start | bytes 786440 | tf_op jit(solution)/shard_map/ppermute | solution.py:106
  13.0 18.0 %copy-start = (bf16[128,1024]{1,0:T(8,128)(2,1)}, bf16[128,1024]{1,0:T(8,128)(2,1)S(1)}, u32[]{:S(2)}) copy-start(bf16[128,1024]{1,0:T(8,128)(2,1)S(1)} %collective-permute-done.3.refs_4_.refs_9_) | copy-start | bytes 786436
  17.8 13.2 %copy-start.1 = (bf16[128,1024]{1,0:T(8,128)(2,1)}, bf16[128,1024]{1,0:T(8,128)(2,1)S(1)}, u32[]{:S(2)}) copy-start(bf16[128,1024]{1,0:T(8,128)(2,1)S(1)} %collective-permute-done.2.refs_3_.refs_8_) | copy-start | bytes 786436
  24.4 6.6 %copy-start.2 = (bf16[128,1024]{1,0:T(8,128)(2,1)}, bf16[128,1024]{1,0:T(8,128)(2,1)S(1)}, u32[]{:S(2)}) copy-start(bf16[128,1024]{1,0:T(8,128)(2,1)S(1)} %collective-permute-done.1.refs_2_.refs_7_) | copy-start | bytes 786436
  31.0 0.7 copy-start.3
  47.4 9.3 %collective-permute-start.4 = (bf16[4,2,128,128]{3,2,1,0:T(8,128)(2,1)}, bf16[4,2,128,128]{3,2,1,0:T(8,128)(2,1)S(1)}, u32[]{:S(2)}, u32[]{:S(2)}) collective-permute-start(bf16[4,2,128,128]{3,2,1,0:T(8,128)(2,1)} %get-tuple-element.16), channel_id=1, source_target_pairs={{1,0},{2,1},{3,2},{4,3},{5,4},{6,5},{7,6},{9,8},{10,9},{11,10},{12... | collective-permute-start | bytes 786440 | tf_op jit(solution)/shard_map/ppermute | solution.py:135
  49.3 24.9 %collective-permute-start.5 = (bf16[4,2,128,128]{3,2,1,0:T(8,128)(2,1)}, bf16[4,2,128,128]{3,2,1,0:T(8,128)(2,1)S(1)}, u32[]{:S(2)}, u32[]{:S(2)}) collective-permute-start(bf16[4,2,128,128]{3,2,1,0:T(8,128)(2,1)} %get-tuple-element.17), channel_id=1, source_target_pairs={{2,0},{3,1},{4,2},{5,3},{6,4},{7,5},{10,8},{11,9},{12,10},{13,11},... | collective-permute-start | bytes 786440 | tf_op jit(solution)/shard_map/ppermute | solution.py:135
  51.2 23.0 %collective-permute-start.6 = (bf16[4,2,128,128]{3,2,1,0:T(8,128)(2,1)}, bf16[4,2,128,128]{3,2,1,0:T(8,128)(2,1)S(1)}, u32[]{:S(2)}, u32[]{:S(2)}) collective-permute-start(bf16[4,2,128,128]{3,2,1,0:T(8,128)(2,1)} %get-tuple-element.18), channel_id=1, source_target_pairs={{3,0},{4,1},{5,2},{6,3},{7,4},{11,8},{12,9},{13,10},{14,11},{15,12... | collective-permute-start | bytes 786440 | tf_op jit(solution)/shard_map/ppermute | solution.py:135
  52.5 21.7 %collective-permute-start.7 = (bf16[4,2,128,128]{3,2,1,0:T(8,128)(2,1)}, bf16[4,2,128,128]{3,2,1,0:T(8,128)(2,1)S(1)}, u32[]{:S(2)}, u32[]{:S(2)}) collective-permute-start(bf16[4,2,128,128]{3,2,1,0:T(8,128)(2,1)} %get-tuple-element.19), channel_id=1, source_target_pairs={{4,0},{5,1},{6,2},{7,3},{12,8},{13,9},{14,10},{15,11},{20,16},{21,... | collective-permute-start | bytes 786440 | tf_op jit(solution)/shard_map/ppermute | solution.py:135
  56.7 17.6 %copy-start.5 = (bf16[4,2,128,128]{3,2,1,0:T(8,128)(2,1)}, bf16[4,2,128,128]{3,2,1,0:T(8,128)(2,1)S(1)}, u32[]{:S(2)}) copy-start(bf16[4,2,128,128]{3,2,1,0:T(8,128)(2,1)S(1)} %collective-permute-done.4.refs_1_) | copy-start | bytes 786436
  74.3 0.7 copy-start.6
  74.3 0.8 %copy-start.7 = (bf16[4,2,128,128]{3,2,1,0:T(8,128)(2,1)}, bf16[4,2,128,128]{3,2,1,0:T(8,128)(2,1)S(1)}, u32[]{:S(2)}) copy-start(bf16[4,2,128,128]{3,2,1,0:T(8,128)(2,1)S(1)} %collective-permute-done.6.refs_3_) | copy-start | bytes 786436
  74.3 0.9 %copy-start.8 = (bf16[4,2,128,128]{3,2,1,0:T(8,128)(2,1)}, bf16[4,2,128,128]{3,2,1,0:T(8,128)(2,1)S(1)}, u32[]{:S(2)}) copy-start(bf16[4,2,128,128]{3,2,1,0:T(8,128)(2,1)S(1)} %collective-permute-done.7.refs_4_) | copy-start | bytes 786436

commit v2 on v1

v2 whole, which is shorter than its diff:
```python
import functools

import jax
import jax.numpy as jnp
from jax import lax
from jax.experimental import pallas as pl
from jax.experimental.pallas import tpu as pltpu
from jax.sharding import PartitionSpec as P


H = 32
KVH = 4
HD = 128
GROUP = 8
SEGS = 16
MOST = 512
SCALE = HD**-0.5
EXP2_SCALE = SCALE * 1.4426950408889634
NEG = -1e30
ROWS = 128
HEADS_AT_ONCE = 2
SIZES = (1, 2, 3, 4)
PIECES = 2
IN_PIECES = 2

NT = (((1,), (1,)), ((), ()))
TN = (((0,), (0,)), ((), ()))


def dot(a, b, dims=(((1,), (0,)), ((), ()))):
    return lax.dot_general(a, b, dims, preferred_element_type=jnp.float32)


def halves(a, b):
    n = a.shape[0] // 2
    return jnp.concatenate([dot(a[:n], b), dot(a[n:], b)], axis=0)


def stack(parts):
    return jnp.concatenate(parts, axis=0)


def attend(chunks, given, lens_ref, where_ref, q_ref, g_ref, *refs):
    refs = refs[given:]
    k_refs, v_refs = refs[:chunks], refs[chunks : 2 * chunks]
    att_ref, dq_ref = refs[2 * chunks : 2 * chunks + 2]
    part_refs = refs[2 * chunks + 2 : 3 * chunks + 2]
    (bias_ref,) = refs[3 * chunks + 2 :]
    run = where_ref[0]
    ends = []
    for d in range(SEGS):
        ends.append(lens_ref[d] + (ends[-1] if d else 0))

    @pl.when(pl.program_id(0) == 0)
    def _():
        pos = run * ROWS + lax.broadcasted_iota(jnp.int32, (ROWS, ROWS), 0)
        lane = lax.broadcasted_iota(jnp.int32, (ROWS, ROWS), 1)
        start = jnp.zeros((ROWS, ROWS), jnp.int32)
        for end in ends:
            start = jnp.where(pos >= end, end, start)
        for c in range(chunks):
            key_pos = (run - c) * ROWS + lane
            seen = (key_pos >= start) & (key_pos <= pos)
            bias_ref[:, c * ROWS : (c + 1) * ROWS] = jnp.where(seen, 0.0, NEG)

    first = jnp.int32(0)
    for end in ends:
        first = jnp.where(run * ROWS >= end, end, first)
    live = run - first // ROWS + 1

    def work(n):
        k = stack([r[...] for r in k_refs[:n]])
        v = stack([r[...] for r in v_refs[:n]])
        v_one = jnp.concatenate([v, jnp.ones((n * ROWS, HD), jnp.bfloat16)], axis=1)
        bias = stack([bias_ref[:, : n * ROWS]] * HEADS_AT_ONCE)
        blocks = range(GROUP // HEADS_AT_ONCE)
        heads = [
            [slice(h * HD, (h + 1) * HD) for h in range(b, b + HEADS_AT_ONCE)]
            for b in range(0, GROUP, HEADS_AT_ONCE)
        ]
        q = [stack([q_ref[:, h] for h in heads[b]]) for b in blocks]
        g = [stack([g_ref[:, h] for h in heads[b]]) for b in blocks]
        expo, weights, g_scaled, rowdot, dscores = ([] for _ in range(5))
        scores = [dot(q[b], k, NT) + bias for b in blocks]
        for b in blocks:
            top = jnp.max(scores[b], axis=1, keepdims=True)
            expo.append(jnp.exp2((scores[b] - top) * EXP2_SCALE))
            weights.append(expo[b].astype(jnp.bfloat16))
        for b in blocks:
            out = halves(weights[b], v_one)
            inv = 1.0 / out[:, HD:]
            att = (out[:, :HD] * inv).astype(jnp.bfloat16)
            wide = g[b].astype(jnp.float32) * inv
            dots = jnp.sum(wide * att.astype(jnp.float32), axis=1, keepdims=True)
            rowdot.append(dots)
            g_scaled.append(wide.astype(jnp.bfloat16))
            for i, h in enumerate(heads[b]):
                att_ref[:, h] = att[i * ROWS : (i + 1) * ROWS]
        for b in blocks:
            dprobs = dot(g_scaled[b], v, NT)
            dscores.append((expo[b] * (dprobs - rowdot[b])).astype(jnp.bfloat16))
        for b in blocks:
            dq = (halves(dscores[b], k) * SCALE).astype(jnp.bfloat16)
            for i, h in enumerate(heads[b]):
                dq_ref[:, h] = dq[i * ROWS : (i + 1) * ROWS]
        dk = dot(stack(q), stack(dscores), TN) * SCALE
        dv = dot(stack(g_scaled), stack(weights), TN)
        for c in range(n):
            cols = slice(c * ROWS, (c + 1) * ROWS)
            part_refs[c][0, 0] = dk[:, cols].astype(jnp.bfloat16)
            part_refs[c][0, 1] = dv[:, cols].astype(jnp.bfloat16)
        for c in range(n, chunks):
            part_refs[c][...] = jnp.zeros_like(part_refs[c])

    sizes = [n for n in SIZES if n < chunks] + [chunks]
    for low, n in zip([0] + sizes, sizes):
        pl.when((live > low) & (live <= n))(functools.partial(work, n))


def total(chunks, *refs):
    part_refs, o_refs = refs[:chunks], refs[-2:]
    for i, o_ref in enumerate(o_refs):
        s = part_refs[0][0, i].astype(jnp.float32)
        for r in part_refs[1:]:
            s = s + r[0, i].astype(jnp.float32)
        o_ref[...] = s.T.astype(jnp.bfloat16)


def total_heads(first, count, parts, before):
    part = pl.BlockSpec((1, 2, HD, ROWS), lambda h: (h, 0, 0, 0))
    out = pl.BlockSpec((ROWS, HD), lambda h: (0, first + h))
    return pl.pallas_call(
        functools.partial(total, len(parts)),
        grid=(count,),
        in_specs=[part] * len(parts)
        + [pl.BlockSpec(memory_space=pl.ANY)] * len(before),
        out_specs=[out, out],
        out_shape=[jax.ShapeDtypeStruct((ROWS, KVH * HD), jnp.bfloat16)] * 2,
        input_output_aliases={len(parts) + i: i for i in range(len(before))},
        cost_estimate=pl.CostEstimate(
            flops=count * 10 * HD * ROWS,
            bytes_accessed=count * 12 * HD * ROWS * 2,
            transcendentals=0,
        ),
        name="total",
    )(*parts, *before)


def attend_heads(first, count, held, lens, run, wide_args, keys, values, got, before):
    chunks = len(got) + 1
    flops = 12 * count * GROUP * ROWS * HD * chunks * ROWS
    wide = pl.BlockSpec((ROWS, GROUP * HD), lambda h, *_: (0, first + h))
    own = pl.BlockSpec((ROWS, HD), lambda h, *_: (0, first + h))
    skip, width = held
    k_spec = pl.BlockSpec((ROWS, HD), lambda h, *_: (0, skip + h))
    v_spec = pl.BlockSpec((ROWS, HD), lambda h, *_: (0, width + skip + h))
    part = pl.BlockSpec((1, 2, HD, ROWS), lambda h, *_: (h, 0, 0, 0))
    part_shape = jax.ShapeDtypeStruct((count, 2, HD, ROWS), jnp.bfloat16)
    big = jax.ShapeDtypeStruct((ROWS, H * HD), jnp.bfloat16)
    back = chunks - 1
    return pl.pallas_call(
        functools.partial(attend, chunks, len(before)),
        grid_spec=pltpu.PrefetchScalarGridSpec(
            num_scalar_prefetch=2,
            grid=(count,),
            in_specs=[wide, wide]
            + [pl.BlockSpec(memory_space=pl.ANY)] * len(before)
            + [own]
            + [k_spec] * back
            + [own]
            + [v_spec] * back,
            out_specs=[wide, wide] + [part] * chunks,
            scratch_shapes=[pltpu.VMEM((ROWS, chunks * ROWS), jnp.float32)],
        ),
        out_shape=[big, big] + [part_shape] * chunks,
        input_output_aliases={4 + i: i for i in range(len(before))},
        cost_estimate=pl.CostEstimate(
            flops=flops,
            bytes_accessed=4 * count * GROUP * ROWS * HD * 2,
            transcendentals=count * GROUP * ROWS * chunks * ROWS,
        ),
        name="attend",
    )(lens, run, *wide_args, *before, keys, *got, values, *got)


def shift(x, by, n):
    pairs = [(i, i + by) for i in range(n) if 0 <= i + by < n]
    return lax.ppermute(x, "seq", pairs)


def shards(queries, keys, values, lengths, out_grad):
    n = lax.axis_size("seq")
    back = min(n - 1, -(-(MOST - 1) // ROWS))
    chunks = back + 1
    run = lax.axis_index("seq").astype(jnp.int32)[None]
    shifts = list(range(back, 0, -1))
    got = {}
    for first in range(0, KVH, KVH // IN_PIECES):
        count = KVH // IN_PIECES
        cols = slice(first * HD, (first + count) * HD)
        both = jnp.concatenate([keys[:, cols], values[:, cols]], axis=1)
        here = {c: shift(both, c, n) for c in shifts}
        for h in range(first, first + count):
            got[h] = (h - first, count), [here[c] for c in range(1, chunks)]
    before, sums = (), ()
    for first in range(0, KVH, KVH // PIECES):
        count = KVH // PIECES
        held, from_left = got[first]
        att, dq, *own = attend_heads(
            first,
            count,
            held,
            lengths[0],
            run,
            (queries, out_grad),
            keys,
            values,
            from_left,
            before,
        )
        before = att, dq
        sent = [shift(own[c], -c, n) for c in range(1, chunks)]
        sums = total_heads(first, count, own[:1] + sent, sums)
    return (*before, *sums)


def solution(mesh):
    rows = P(("dp", "seq"), None)
    return jax.shard_map(
        shards,
        mesh=mesh,
        in_specs=(rows, rows, rows, P("dp", None), rows),
        out_specs=(rows,) * 4,
        check_vma=False,
    )
```

time: 77.7 us -> 63.9 us (0.82)
  the two profiles are of different devices: /device:TPU:450 before, /device:TPU:322 now
where the time goes in v2:
time: 63.9 us; the launch traced here: 63.1 us
  starting transfers between devices  34.5 us (54%)
  Pallas kernels  15.6 us (24%)
  waiting for transfers between devices  8.39 us (13%)
  local copies, waits for them, and re-layouts  3.51 us (5%)
  between operations  1.06 us (2%)
    ppermute x16, starting transfers between devices, shift(): return lax.ppermute(x, 'seq', pairs)  34.5 us
    pallas_call x2, Pallas kernels, attend_heads(): pl.pallas_call(functools.partial(attend, chunks, len(before)), grid_spec=...  11.9 us
    ppermute x16, waiting for transfers between devices, shift(): return lax.ppermute(x, 'seq', pairs)  8.39 us
    pallas_call x2, Pallas kernels, total_heads(): pl.pallas_call(functools.partial(total, len(parts)), grid=(count,), in_sp...  3.73 us
    unnamed x32, local copies, waits for them, and re-layouts  2.55 us
  transfers between devices with their start and end apart: 16, of which 2 were waited for; matrix products, arithmetic and copies ran while one was open for 0% of the time, Pallas kernels for 22%

profile of v2, /device:TPU:322, one launch (start us, length us, event | category | flops | bytes accessed | tf_op | source)
XLA Modules:
  0.0 63.1 jit_solution(13078804468669994105)
XLA Ops:
  0.6 1.0 %fusion = (bf16[128,256]{1,0:T(8,128)(2,1)S(1)}, bf16[128,256]{1,0:T(8,128)(2,1)S(1)}, bf16[128,256]{1,0:T(8,128)(2,1)S(1)}, bf16[128,256]{1,0:T(8,128)(2,1)S(1)}) fusion(bf16[128,512]{1,0:T(8,128)(2,1)} %refs_2_.1, bf16[128,512]{1,0:T(8,128)(2,1)} %refs_7_.1), kind=kLoop, calls=%fused_computation.2 | loop fusion | bytes 524288 | tf_op jit(solution)/shard_map/slice | solution.py:201
  1.6 3.5 %collective-permute-start = (bf16[128,512]{1,0:T(8,128)(2,1)S(1)}, bf16[128,512]{1,0:T(8,128)(2,1)S(1)}, u32[]{:S(2)}, u32[]{:S(2)}) collective-permute-start(bf16[128,512]{1,0:T(8,128)(2,1)S(1)} %pad_maximum_fusion), channel_id=1, source_target_pairs={{0,1},{1,2},{2,3},{3,4},{4,5},{5,6},{6,7},{8,9},{9,10},{10,11},{11... | collective-permute-start | bytes 393224 | tf_op jit(solution)/shard_map/ppermute | solution.py:188
  5.1 3.4 %collective-permute-start.1 = (bf16[128,512]{1,0:T(8,128)(2,1)S(1)}, bf16[128,512]{1,0:T(8,128)(2,1)S(1)}, u32[]{:S(2)}, u32[]{:S(2)}) collective-permute-start(bf16[128,512]{1,0:T(8,128)(2,1)S(1)} %pad_maximum_fusion), channel_id=1, source_target_pairs={{0,2},{1,3},{2,4},{3,5},{4,6},{5,7},{8,10},{9,11},{10,12},{11,13},... | collective-permute-start | bytes 393224 | tf_op jit(solution)/shard_map/ppermute | solution.py:188
  8.5 2.4 %collective-permute-start.2 = (bf16[128,512]{1,0:T(8,128)(2,1)S(1)}, bf16[128,512]{1,0:T(8,128)(2,1)S(1)}, u32[]{:S(2)}, u32[]{:S(2)}) collective-permute-start(bf16[128,512]{1,0:T(8,128)(2,1)S(1)} %pad_maximum_fusion), channel_id=1, source_target_pairs={{0,3},{1,4},{2,5},{3,6},{4,7},{8,11},{9,12},{10,13},{11,14},{12,15... | collective-permute-start | bytes 393224 | tf_op jit(solution)/shard_map/ppermute | solution.py:188
  11.0 1.3 %collective-permute-start.3 = (bf16[128,512]{1,0:T(8,128)(2,1)S(1)}, bf16[128,512]{1,0:T(8,128)(2,1)S(1)}, u32[]{:S(2)}, u32[]{:S(2)}) collective-permute-start(bf16[128,512]{1,0:T(8,128)(2,1)S(1)} %pad_maximum_fusion), channel_id=1, source_target_pairs={{0,4},{1,5},{2,6},{3,7},{8,12},{9,13},{10,14},{11,15},{16,20},{17,... | collective-permute-start | bytes 393224 | tf_op jit(solution)/shard_map/ppermute | solution.py:188
  12.3 2.9 %collective-permute-start.4 = (bf16[128,512]{1,0:T(8,128)(2,1)S(1)}, bf16[128,512]{1,0:T(8,128)(2,1)S(1)}, u32[]{:S(2)}, u32[]{:S(2)}) collective-permute-start(bf16[128,512]{1,0:T(8,128)(2,1)S(1)} %pad_maximum_fusion.1), channel_id=1, source_target_pairs={{0,1},{1,2},{2,3},{3,4},{4,5},{5,6},{6,7},{8,9},{9,10},{10,11},{11... | collective-permute-start | bytes 393224 | tf_op jit(solution)/shard_map/ppermute | solution.py:188
  15.1 0.0 collective-permute-done.refs_1_.refs_6_
  15.2 0.0 copy-start.11
  15.2 1.9 %collective-permute-start.5 = (bf16[128,512]{1,0:T(8,128)(2,1)S(1)}, bf16[128,512]{1,0:T(8,128)(2,1)S(1)}, u32[]{:S(2)}, u32[]{:S(2)}) collective-permute-start(bf16[128,512]{1,0:T(8,128)(2,1)S(1)} %pad_maximum_fusion.1), channel_id=1, source_target_pairs={{0,2},{1,3},{2,4},{3,5},{4,6},{5,7},{8,10},{9,11},{10,12},{11,13},... | collective-permute-start | bytes 393224 | tf_op jit(solution)/shard_map/ppermute | solution.py:188
  17.1 0.0 collective-permute-done.1.refs_2_.refs_7_
  17.1 0.0 copy-start.13
  17.1 1.3 %collective-permute-start.6 = (bf16[128,512]{1,0:T(8,128)(2,1)S(1)}, bf16[128,512]{1,0:T(8,128)(2,1)S(1)}, u32[]{:S(2)}, u32[]{:S(2)}) collective-permute-start(bf16[128,512]{1,0:T(8,128)(2,1)S(1)} %pad_maximum_fusion.1), channel_id=1, source_target_pairs={{0,3},{1,4},{2,5},{3,6},{4,7},{8,11},{9,12},{10,13},{11,14},{12,15... | collective-permute-start | bytes 393224 | tf_op jit(solution)/shard_map/ppermute | solution.py:188
  18.4 0.0 collective-permute-done.2.refs_3_.refs_8_
  18.4 3.4 %collective-permute-start.7 = (bf16[128,512]{1,0:T(8,128)(2,1)S(1)}, bf16[128,512]{1,0:T(8,128)(2,1)S(1)}, u32[]{:S(2)}, u32[]{:S(2)}) collective-permute-start(bf16[128,512]{1,0:T(8,128)(2,1)S(1)} %pad_maximum_fusion.1), channel_id=1, source_target_pairs={{0,4},{1,5},{2,6},{3,7},{8,12},{9,13},{10,14},{11,15},{16,20},{17,... | collective-permute-start | bytes 393224 | tf_op jit(solution)/shard_map/ppermute | solution.py:188
  21.8 0.0 collective-permute-done.3.refs_4_.refs_9_
  21.9 0.6 copy-done.15
  22.5 5.9 %attend.2 = (bf16[128,4096]{1,0:T(8,128)(2,1)}, bf16[128,4096]{1,0:T(8,128)(2,1)}, bf16[2,2,128,128]{3,2,1,0:T(8,128)(2,1)}, bf16[2,2,128,128]{3,2,1,0:T(8,128)(...) custom-call(s32[16]{0:T(128)} %bitcast.2, ...), custom_call_target="tpu_custom_call" | custom-call | flops 2013265920 | bytes 2097152 | tf_op jit(solution)/shard_map/attend/pallas_call | solution.py:161
  28.4 2.2 %collective-permute-start.12 = (bf16[2,2,128,128]{3,2,1,0:T(8,128)(2,1)}, bf16[2,2,128,128]{3,2,1,0:T(8,128)(2,1)S(1)}, u32[]{:S(2)}, u32[]{:S(2)}) collective-permute-start(bf16[2,2,128,128]{3,2,1,0:T(8,128)(2,1)} %get-tuple-element.32), channel_id=1, source_target_pairs={{1,0},{2,1},{3,2},{4,3},{5,4},{6,5},{7,6},{9,8},{10,9},{11,10},{12... | collective-permute-start | bytes 393224 | tf_op jit(solution)/shard_map/ppermute | solution.py:188
  30.7 0.0 collective-permute-done.4.refs_3_.refs_8_
  30.7 0.0 copy-start.8
  30.7 2.5 %collective-permute-start.13 = (bf16[2,2,128,128]{3,2,1,0:T(8,128)(2,1)}, bf16[2,2,128,128]{3,2,1,0:T(8,128)(2,1)S(1)}, u32[]{:S(2)}, u32[]{:S(2)}) collective-permute-start(bf16[2,2,128,128]{3,2,1,0:T(8,128)(2,1)} %get-tuple-element.33), channel_id=1, source_target_pairs={{2,0},{3,1},{4,2},{5,3},{6,4},{7,5},{10,8},{11,9},{12,10},{13,11},... | collective-permute-start | bytes 393224 | tf_op jit(solution)/shard_map/ppermute | solution.py:188
  33.2 0.0 collective-permute-done.5.refs_4_.refs_9_
  33.2 0.0 copy-start.9
  33.3 1.3 %collective-permute-start.14 = (bf16[2,2,128,128]{3,2,1,0:T(8,128)(2,1)}, bf16[2,2,128,128]{3,2,1,0:T(8,128)(2,1)S(1)}, u32[]{:S(2)}, u32[]{:S(2)}) collective-permute-start(bf16[2,2,128,128]{3,2,1,0:T(8,128)(2,1)} %get-tuple-element.34), channel_id=1, source_target_pairs={{3,0},{4,1},{5,2},{6,3},{7,4},{11,8},{12,9},{13,10},{14,11},{15,12... | collective-permute-start | bytes 393224 | tf_op jit(solution)/shard_map/ppermute | solution.py:188
  34.6 0.0 collective-permute-done.6.refs_5_.refs_10_
  34.6 1.5 %collective-permute-start.15 = (bf16[2,2,128,128]{3,2,1,0:T(8,128)(2,1)}, bf16[2,2,128,128]{3,2,1,0:T(8,128)(2,1)S(1)}, u32[]{:S(2)}, u32[]{:S(2)}) collective-permute-start(bf16[2,2,128,128]{3,2,1,0:T(8,128)(2,1)} %get-tuple-element.35), channel_id=1, source_target_pairs={{4,0},{5,1},{6,2},{7,3},{12,8},{13,9},{14,10},{15,11},{20,16},{21,... | collective-permute-start | bytes 393224 | tf_op jit(solution)/shard_map/ppermute | solution.py:188
  36.1 0.0 collective-permute-done.7.refs_6_.refs_11_
  36.1 0.0 copy-start.12
  36.1 0.0 copy-done.8
  36.1 0.0 copy-done.9
  36.1 0.6 copy-done.12
  36.7 6.0 %attend.3 = (bf16[128,4096]{1,0:T(8,128)(2,1)}, bf16[128,4096]{1,0:T(8,128)(2,1)}, bf16[2,2,128,128]{3,2,1,0:T(8,128)(2,1)}, bf16[2,2,128,128]{3,2,1,0:T(8,128)(...) custom-call(s32[16]{0:T(128)} %bitcast.3, ...), custom_call_target="tpu_custom_call", output_to_operand_aliasing={{0}: (4, {}), {1}: (5, {})} | custom-call | flops 2013265920 | bytes 2097152 | tf_op jit(solution)/shard_map/attend/pallas_call | solution.py:161
  42.7 1.3 %collective-permute-start.10 = (bf16[2,2,128,128]{3,2,1,0:T(8,128)(2,1)}, bf16[2,2,128,128]{3,2,1,0:T(8,128)(2,1)S(1)}, u32[]{:S(2)}, u32[]{:S(2)}) collective-permute-start(bf16[2,2,128,128]{3,2,1,0:T(8,128)(2,1)} %get-tuple-element.29), channel_id=1, source_target_pairs={{3,0},{4,1},{5,2},{6,3},{7,4},{11,8},{12,9},{13,10},{14,11},{15,12... | collective-permute-start | bytes 393224 | tf_op jit(solution)/shard_map/ppermute | solution.py:188
  44.0 0.0 collective-permute-done.12.refs_1_
  44.0 1.3 %collective-permute-start.11 = (bf16[2,2,128,128]{3,2,1,0:T(8,128)(2,1)}, bf16[2,2,128,128]{3,2,1,0:T(8,128)(2,1)S(1)}, u32[]{:S(2)}, u32[]{:S(2)}) collective-permute-start(bf16[2,2,128,128]{3,2,1,0:T(8,128)(2,1)} %get-tuple-element.30), channel_id=1, source_target_pairs={{4,0},{5,1},{6,2},{7,3},{12,8},{13,9},{14,10},{15,11},{20,16},{21,... | collective-permute-start | bytes 393224 | tf_op jit(solution)/shard_map/ppermute | solution.py:188
  45.3 0.0 collective-permute-done.13.refs_2_
  45.3 2.4 %collective-permute-start.8 = (bf16[2,2,128,128]{3,2,1,0:T(8,128)(2,1)}, bf16[2,2,128,128]{3,2,1,0:T(8,128)(2,1)S(1)}, u32[]{:S(2)}, u32[]{:S(2)}) collective-permute-start(bf16[2,2,128,128]{3,2,1,0:T(8,128)(2,1)} %get-tuple-element.27), channel_id=1, source_target_pairs={{1,0},{2,1},{3,2},{4,3},{5,4},{6,5},{7,6},{9,8},{10,9},{11,10},{12... | collective-permute-start | bytes 393224 | tf_op jit(solution)/shard_map/ppermute | solution.py:188
  47.8 0.0 collective-permute-done.14.refs_3_
  47.8 1.9 %collective-permute-start.9 = (bf16[2,2,128,128]{3,2,1,0:T(8,128)(2,1)}, bf16[2,2,128,128]{3,2,1,0:T(8,128)(2,1)S(1)}, u32[]{:S(2)}, u32[]{:S(2)}) collective-permute-start(bf16[2,2,128,128]{3,2,1,0:T(8,128)(2,1)} %get-tuple-element.28), channel_id=1, source_target_pairs={{2,0},{3,1},{4,2},{5,3},{6,4},{7,5},{10,8},{11,9},{12,10},{13,11},... | collective-permute-start | bytes 393224 | tf_op jit(solution)/shard_map/ppermute | solution.py:188
  49.7 0.0 collective-permute-done.15.refs_4_
  49.8 0.6 copy-done.3
  50.4 1.9 %total.2 = (bf16[128,512]{1,0:T(8,128)(2,1)}, bf16[128,512]{1,0:T(8,128)(2,1)}) custom-call(bf16[2,2,128,128]{3,2,1,0:T(8,128)(2,1)} %get-tuple-element.31.refs_0_, bf16[2,2,128,128]{3,2,1,0:T(8,128)(2,1)} %copy-done, bf16[2,2,128,128]{3,2,1,0:T(8,128)(2,1)} %copy-done.1, bf16[2,2,128,128]{3,2,1,0:T(8,128)(2,1)} %copy-done.2, bf16[2,2,128,128]{3,2,1,0:T(8,128)(2,1)} %copy-done.3), custom_call_target="tpu_custom_call" | custom-call | flops 327680 | bytes 786432 | tf_op jit(solution)/shard_map/total/pallas_call | solution.py:132
  52.3 0.0 collective-permute-done.10.refs_3_
  52.3 6.2 %collective-permute-done.11.refs_4_ = bf16[2,2,128,128]{3,2,1,0:T(8,128)(2,1)S(1)} collective-permute-done((bf16[2,2,128,128]{3,2,1,0:T(8,128)(2,1)}, bf16[2,2,128,128]{3,2,1,0:T(8,128)(2,1)S(1)}, u32[]{:S(2)}, u32[]{:S(2)}) %collective-permute-start.11) | collective-permute-done | bytes 131104 | tf_op jit(solution)/shard_map/ppermute | solution.py:188
  58.5 0.0 collective-permute-done.8.refs_1_
  58.5 2.2 %collective-permute-done.9.refs_2_ = bf16[2,2,128,128]{3,2,1,0:T(8,128)(2,1)S(1)} collective-permute-done((bf16[2,2,128,128]{3,2,1,0:T(8,128)(2,1)}, bf16[2,2,128,128]{3,2,1,0:T(8,128)(2,1)S(1)}, u32[]{:S(2)}, u32[]{:S(2)}) %collective-permute-start.9) | collective-permute-done | bytes 131104 | tf_op jit(solution)/shard_map/ppermute | solution.py:188
  60.6 0.6 %copy-done.7 = bf16[2,2,128,128]{3,2,1,0:T(8,128)(2,1)} copy-done((bf16[2,2,128,128]{3,2,1,0:T(8,128)(2,1)}, bf16[2,2,128,128]{3,2,1,0:T(8,128)(2,1)S(1)}, u32[]{:S(2)}) %copy-start.7) | copy-done | bytes 131096
  61.3 1.9 %total.3 = (bf16[128,512]{1,0:T(8,128)(2,1)}, bf16[128,512]{1,0:T(8,128)(2,1)}) custom-call(bf16[2,2,128,128]{3,2,1,0:T(8,128)(2,1)} %get-tuple-element.26.refs_0_, bf16[2,2,128,128]{3,2,1,0:T(8,128)(2,1)} %copy-done.6, bf16[2,2,128,128]{3,2,1,0:T(8,128)(2,1)} %copy-done.7, ...), custom_call_target="tpu_custom_call", output_to_operand_aliasing={{0}: (5, {}), {1}: (6, {})} | custom-call | flops 327680 | bytes 786432 | tf_op jit(solution)/shard_map/total/pallas_call | solution.py:132
  (23 shorter events, 0.1 us)
Async XLA Ops:
  1.6 13.5 %collective-permute-start = (bf16[128,512]{1,0:T(8,128)(2,1)S(1)}, bf16[128,512]{1,0:T(8,128)(2,1)S(1)}, u32[]{:S(2)}, u32[]{:S(2)}) collective-permute-start(bf16[128,512]{1,0:T(8,128)(2,1)S(1)} %pad_maximum_fusion), channel_id=1, source_target_pairs={{0,1},{1,2},{2,3},{3,4},{4,5},{5,6},{6,7},{8,9},{9,10},{10,11},{11... | collective-permute-start | bytes 393224 | tf_op jit(solution)/shard_map/ppermute | solution.py:188
  5.1 12.0 %collective-permute-start.1 = (bf16[128,512]{1,0:T(8,128)(2,1)S(1)}, bf16[128,512]{1,0:T(8,128)(2,1)S(1)}, u32[]{:S(2)}, u32[]{:S(2)}) collective-permute-start(bf16[128,512]{1,0:T(8,128)(2,1)S(1)} %pad_maximum_fusion), channel_id=1, source_target_pairs={{0,2},{1,3},{2,4},{3,5},{4,6},{5,7},{8,10},{9,11},{10,12},{11,13},... | collective-permute-start | bytes 393224 | tf_op jit(solution)/shard_map/ppermute | solution.py:188
  8.5 9.9 %collective-permute-start.2 = (bf16[128,512]{1,0:T(8,128)(2,1)S(1)}, bf16[128,512]{1,0:T(8,128)(2,1)S(1)}, u32[]{:S(2)}, u32[]{:S(2)}) collective-permute-start(bf16[128,512]{1,0:T(8,128)(2,1)S(1)} %pad_maximum_fusion), channel_id=1, source_target_pairs={{0,3},{1,4},{2,5},{3,6},{4,7},{8,11},{9,12},{10,13},{11,14},{12,15... | collective-permute-start | bytes 393224 | tf_op jit(solution)/shard_map/ppermute | solution.py:188
  11.0 10.9 %collective-permute-start.3 = (bf16[128,512]{1,0:T(8,128)(2,1)S(1)}, bf16[128,512]{1,0:T(8,128)(2,1)S(1)}, u32[]{:S(2)}, u32[]{:S(2)}) collective-permute-start(bf16[128,512]{1,0:T(8,128)(2,1)S(1)} %pad_maximum_fusion), channel_id=1, source_target_pairs={{0,4},{1,5},{2,6},{3,7},{8,12},{9,13},{10,14},{11,15},{16,20},{17,... | collective-permute-start | bytes 393224 | tf_op jit(solution)/shard_map/ppermute | solution.py:188
  12.3 18.4 %collective-permute-start.4 = (bf16[128,512]{1,0:T(8,128)(2,1)S(1)}, bf16[128,512]{1,0:T(8,128)(2,1)S(1)}, u32[]{:S(2)}, u32[]{:S(2)}) collective-permute-start(bf16[128,512]{1,0:T(8,128)(2,1)S(1)} %pad_maximum_fusion.1), channel_id=1, source_target_pairs={{0,1},{1,2},{2,3},{3,4},{4,5},{5,6},{6,7},{8,9},{9,10},{10,11},{11... | collective-permute-start | bytes 393224 | tf_op jit(solution)/shard_map/ppermute | solution.py:188
  15.2 6.7 %copy-start.11 = (bf16[128,512]{1,0:T(8,128)(2,1)}, bf16[128,512]{1,0:T(8,128)(2,1)S(1)}, u32[]{:S(2)}) copy-start(bf16[128,512]{1,0:T(8,128)(2,1)S(1)} %collective-permute-done.refs_1_.refs_6_) | copy-start | bytes 393220
  15.2 18.1 %collective-permute-start.5 = (bf16[128,512]{1,0:T(8,128)(2,1)S(1)}, bf16[128,512]{1,0:T(8,128)(2,1)S(1)}, u32[]{:S(2)}, u32[]{:S(2)}) collective-permute-start(bf16[128,512]{1,0:T(8,128)(2,1)S(1)} %pad_maximum_fusion.1), channel_id=1, source_target_pairs={{0,2},{1,3},{2,4},{3,5},{4,6},{5,7},{8,10},{9,11},{10,12},{11,13},... | collective-permute-start | bytes 393224 | tf_op jit(solution)/shard_map/ppermute | solution.py:188
  17.1 4.8 %copy-start.13 = (bf16[128,512]{1,0:T(8,128)(2,1)}, bf16[128,512]{1,0:T(8,128)(2,1)S(1)}, u32[]{:S(2)}) copy-start(bf16[128,512]{1,0:T(8,128)(2,1)S(1)} %collective-permute-done.1.refs_2_.refs_7_) | copy-start | bytes 393220
  17.1 17.4 %collective-permute-start.6 = (bf16[128,512]{1,0:T(8,128)(2,1)S(1)}, bf16[128,512]{1,0:T(8,128)(2,1)S(1)}, u32[]{:S(2)}, u32[]{:S(2)}) collective-permute-start(bf16[128,512]{1,0:T(8,128)(2,1)S(1)} %pad_maximum_fusion.1), channel_id=1, source_target_pairs={{0,3},{1,4},{2,5},{3,6},{4,7},{8,11},{9,12},{10,13},{11,14},{12,15... | collective-permute-start | bytes 393224 | tf_op jit(solution)/shard_map/ppermute | solution.py:188
  18.4 3.4 %copy-start.14 = (bf16[128,512]{1,0:T(8,128)(2,1)}, bf16[128,512]{1,0:T(8,128)(2,1)S(1)}, u32[]{:S(2)}) copy-start(bf16[128,512]{1,0:T(8,128)(2,1)S(1)} %collective-permute-done.2.refs_3_.refs_8_) | copy-start | bytes 393220
  18.4 17.6 %collective-permute-start.7 = (bf16[128,512]{1,0:T(8,128)(2,1)S(1)}, bf16[128,512]{1,0:T(8,128)(2,1)S(1)}, u32[]{:S(2)}, u32[]{:S(2)}) collective-permute-start(bf16[128,512]{1,0:T(8,128)(2,1)S(1)} %pad_maximum_fusion.1), channel_id=1, source_target_pairs={{0,4},{1,5},{2,6},{3,7},{8,12},{9,13},{10,14},{11,15},{16,20},{17,... | collective-permute-start | bytes 393224 | tf_op jit(solution)/shard_map/ppermute | solution.py:188
  21.8 0.6 %copy-start.15 = (bf16[128,512]{1,0:T(8,128)(2,1)}, bf16[128,512]{1,0:T(8,128)(2,1)S(1)}, u32[]{:S(2)}) copy-start(bf16[128,512]{1,0:T(8,128)(2,1)S(1)} %collective-permute-done.3.refs_4_.refs_9_) | copy-start | bytes 393220
  28.4 15.6 %collective-permute-start.12 = (bf16[2,2,128,128]{3,2,1,0:T(8,128)(2,1)}, bf16[2,2,128,128]{3,2,1,0:T(8,128)(2,1)S(1)}, u32[]{:S(2)}, u32[]{:S(2)}) collective-permute-start(bf16[2,2,128,128]{3,2,1,0:T(8,128)(2,1)} %get-tuple-element.32), channel_id=1, source_target_pairs={{1,0},{2,1},{3,2},{4,3},{5,4},{6,5},{7,6},{9,8},{10,9},{11,10},{12... | collective-permute-start | bytes 393224 | tf_op jit(solution)/shard_map/ppermute | solution.py:188
  30.7 5.4 %copy-start.8 = (bf16[128,512]{1,0:T(8,128)(2,1)}, bf16[128,512]{1,0:T(8,128)(2,1)S(1)}, u32[]{:S(2)}) copy-start(bf16[128,512]{1,0:T(8,128)(2,1)S(1)} %collective-permute-done.4.refs_3_.refs_8_) | copy-start | bytes 393220
  30.7 14.6 %collective-permute-start.13 = (bf16[2,2,128,128]{3,2,1,0:T(8,128)(2,1)}, bf16[2,2,128,128]{3,2,1,0:T(8,128)(2,1)S(1)}, u32[]{:S(2)}, u32[]{:S(2)}) collective-permute-start(bf16[2,2,128,128]{3,2,1,0:T(8,128)(2,1)} %get-tuple-element.33), channel_id=1, source_target_pairs={{2,0},{3,1},{4,2},{5,3},{6,4},{7,5},{10,8},{11,9},{12,10},{13,11},... | collective-permute-start | bytes 393224 | tf_op jit(solution)/shard_map/ppermute | solution.py:188
  33.2 2.8 %copy-start.9 = (bf16[128,512]{1,0:T(8,128)(2,1)}, bf16[128,512]{1,0:T(8,128)(2,1)S(1)}, u32[]{:S(2)}) copy-start(bf16[128,512]{1,0:T(8,128)(2,1)S(1)} %collective-permute-done.5.refs_4_.refs_9_) | copy-start | bytes 393220
  33.3 14.5 %collective-permute-start.14 = (bf16[2,2,128,128]{3,2,1,0:T(8,128)(2,1)}, bf16[2,2,128,128]{3,2,1,0:T(8,128)(2,1)S(1)}, u32[]{:S(2)}, u32[]{:S(2)}) collective-permute-start(bf16[2,2,128,128]{3,2,1,0:T(8,128)(2,1)} %get-tuple-element.34), channel_id=1, source_target_pairs={{3,0},{4,1},{5,2},{6,3},{7,4},{11,8},{12,9},{13,10},{14,11},{15,12... | collective-permute-start | bytes 393224 | tf_op jit(solution)/shard_map/ppermute | solution.py:188
  34.6 1.5 %copy-start.10 = (bf16[128,512]{1,0:T(8,128)(2,1)}, bf16[128,512]{1,0:T(8,128)(2,1)S(1)}, u32[]{:S(2)}) copy-start(bf16[128,512]{1,0:T(8,128)(2,1)S(1)} %collective-permute-done.6.refs_5_.refs_10_) | copy-start | bytes 393220
  34.6 15.1 %collective-permute-start.15 = (bf16[2,2,128,128]{3,2,1,0:T(8,128)(2,1)}, bf16[2,2,128,128]{3,2,1,0:T(8,128)(2,1)S(1)}, u32[]{:S(2)}, u32[]{:S(2)}) collective-permute-start(bf16[2,2,128,128]{3,2,1,0:T(8,128)(2,1)} %get-tuple-element.35), channel_id=1, source_target_pairs={{4,0},{5,1},{6,2},{7,3},{12,8},{13,9},{14,10},{15,11},{20,16},{21,... | collective-permute-start | bytes 393224 | tf_op jit(solution)/shard_map/ppermute | solution.py:188
  36.1 0.7 %copy-start.12 = (bf16[128,512]{1,0:T(8,128)(2,1)}, bf16[128,512]{1,0:T(8,128)(2,1)S(1)}, u32[]{:S(2)}) copy-start(bf16[128,512]{1,0:T(8,128)(2,1)S(1)} %collective-permute-done.7.refs_6_.refs_11_) | copy-start | bytes 393220
  42.7 9.6 %collective-permute-start.10 = (bf16[2,2,128,128]{3,2,1,0:T(8,128)(2,1)}, bf16[2,2,128,128]{3,2,1,0:T(8,128)(2,1)S(1)}, u32[]{:S(2)}, u32[]{:S(2)}) collective-permute-start(bf16[2,2,128,128]{3,2,1,0:T(8,128)(2,1)} %get-tuple-element.29), channel_id=1, source_target_pairs={{3,0},{4,1},{5,2},{6,3},{7,4},{11,8},{12,9},{13,10},{14,11},{15,12... | collective-permute-start | bytes 393224 | tf_op jit(solution)/shard_map/ppermute | solution.py:188
  44.0 5.7 %copy-start = (bf16[2,2,128,128]{3,2,1,0:T(8,128)(2,1)}, bf16[2,2,128,128]{3,2,1,0:T(8,128)(2,1)S(1)}, u32[]{:S(2)}) copy-start(bf16[2,2,128,128]{3,2,1,0:T(8,128)(2,1)S(1)} %collective-permute-done.12.refs_1_) | copy-start | bytes 393220
  44.0 14.4 %collective-permute-start.11 = (bf16[2,2,128,128]{3,2,1,0:T(8,128)(2,1)}, bf16[2,2,128,128]{3,2,1,0:T(8,128)(2,1)S(1)}, u32[]{:S(2)}, u32[]{:S(2)}) collective-permute-start(bf16[2,2,128,128]{3,2,1,0:T(8,128)(2,1)} %get-tuple-element.30), channel_id=1, source_target_pairs={{4,0},{5,1},{6,2},{7,3},{12,8},{13,9},{14,10},{15,11},{20,16},{21,... | collective-permute-start | bytes 393224 | tf_op jit(solution)/shard_map/ppermute | solution.py:188
  45.3 4.4 %copy-start.1 = (bf16[2,2,128,128]{3,2,1,0:T(8,128)(2,1)}, bf16[2,2,128,128]{3,2,1,0:T(8,128)(2,1)S(1)}, u32[]{:S(2)}) copy-start(bf16[2,2,128,128]{3,2,1,0:T(8,128)(2,1)S(1)} %collective-permute-done.13.refs_2_) | copy-start | bytes 393220
  45.3 13.1 %collective-permute-start.8 = (bf16[2,2,128,128]{3,2,1,0:T(8,128)(2,1)}, bf16[2,2,128,128]{3,2,1,0:T(8,128)(2,1)S(1)}, u32[]{:S(2)}, u32[]{:S(2)}) collective-permute-start(bf16[2,2,128,128]{3,2,1,0:T(8,128)(2,1)} %get-tuple-element.27), channel_id=1, source_target_pairs={{1,0},{2,1},{3,2},{4,3},{5,4},{6,5},{7,6},{9,8},{10,9},{11,10},{12... | collective-permute-start | bytes 393224 | tf_op jit(solution)/shard_map/ppermute | solution.py:188
  47.8 2.0 %copy-start.2 = (bf16[2,2,128,128]{3,2,1,0:T(8,128)(2,1)}, bf16[2,2,128,128]{3,2,1,0:T(8,128)(2,1)S(1)}, u32[]{:S(2)}) copy-start(bf16[2,2,128,128]{3,2,1,0:T(8,128)(2,1)S(1)} %collective-permute-done.14.refs_3_) | copy-start | bytes 393220
  47.8 12.8 %collective-permute-start.9 = (bf16[2,2,128,128]{3,2,1,0:T(8,128)(2,1)}, bf16[2,2,128,128]{3,2,1,0:T(8,128)(2,1)S(1)}, u32[]{:S(2)}, u32[]{:S(2)}) collective-permute-start(bf16[2,2,128,128]{3,2,1,0:T(8,128)(2,1)} %get-tuple-element.28), channel_id=1, source_target_pairs={{2,0},{3,1},{4,2},{5,3},{6,4},{7,5},{10,8},{11,9},{12,10},{13,11},... | collective-permute-start | bytes 393224 | tf_op jit(solution)/shard_map/ppermute | solution.py:188
  49.7 0.7 %copy-start.3 = (bf16[2,2,128,128]{3,2,1,0:T(8,128)(2,1)}, bf16[2,2,128,128]{3,2,1,0:T(8,128)(2,1)S(1)}, u32[]{:S(2)}) copy-start(bf16[2,2,128,128]{3,2,1,0:T(8,128)(2,1)S(1)} %collective-permute-done.15.refs_4_) | copy-start | bytes 393220
  52.3 8.4 %copy-start.4 = (bf16[2,2,128,128]{3,2,1,0:T(8,128)(2,1)}, bf16[2,2,128,128]{3,2,1,0:T(8,128)(2,1)S(1)}, u32[]{:S(2)}) copy-start(bf16[2,2,128,128]{3,2,1,0:T(8,128)(2,1)S(1)} %collective-permute-done.10.refs_3_) | copy-start | bytes 393220
  58.4 2.2 %copy-start.5 = (bf16[2,2,128,128]{3,2,1,0:T(8,128)(2,1)}, bf16[2,2,128,128]{3,2,1,0:T(8,128)(2,1)S(1)}, u32[]{:S(2)}) copy-start(bf16[2,2,128,128]{3,2,1,0:T(8,128)(2,1)S(1)} %collective-permute-done.11.refs_4_) | copy-start | bytes 393220
  58.5 2.2 %copy-start.6 = (bf16[2,2,128,128]{3,2,1,0:T(8,128)(2,1)}, bf16[2,2,128,128]{3,2,1,0:T(8,128)(2,1)S(1)}, u32[]{:S(2)}) copy-start(bf16[2,2,128,128]{3,2,1,0:T(8,128)(2,1)S(1)} %collective-permute-done.8.refs_1_) | copy-start | bytes 393220
  60.6 0.7 %copy-start.7 = (bf16[2,2,128,128]{3,2,1,0:T(8,128)(2,1)}, bf16[2,2,128,128]{3,2,1,0:T(8,128)(2,1)S(1)}, u32[]{:S(2)}) copy-start(bf16[2,2,128,128]{3,2,1,0:T(8,128)(2,1)S(1)} %collective-permute-done.9.refs_2_) | copy-start | bytes 393220

commit v3 on v2

--- a/solution.py
+++ b/solution.py
@@ -20,6 +20,7 @@
 ROWS = 128
 HEADS_AT_ONCE = 2
 SIZES = (1, 2, 3, 4)
+VMEM_LIMIT = 48 * 2**20
 PIECES = 2
 IN_PIECES = 2
 
@@ -40,13 +41,18 @@
     return jnp.concatenate(parts, axis=0)
 
 
-def attend(chunks, given, lens_ref, where_ref, q_ref, g_ref, *refs):
+def attend(chunks, given, held, lens_ref, where_ref, q_ref, g_ref, *refs):
     refs = refs[given:]
-    k_refs, v_refs = refs[:chunks], refs[chunks : 2 * chunks]
-    att_ref, dq_ref = refs[2 * chunks : 2 * chunks + 2]
-    part_refs = refs[2 * chunks + 2 : 3 * chunks + 2]
-    (bias_ref,) = refs[3 * chunks + 2 :]
+    kv_refs = refs[:chunks]
+    att_ref, dq_ref = refs[chunks : chunks + 2]
+    part_refs = refs[chunks + 2 : 2 * chunks + 2]
+    (bias_ref,) = refs[2 * chunks + 2 :]
     run = where_ref[0]
+    head, (skip, width) = pl.program_id(0), held
+
+    def at(block, cols=slice(0, HD)):
+        return pl.ds(pl.multiple_of(block * HD + cols.start, HD), HD)
+
     ends = []
     for d in range(SEGS):
         ends.append(lens_ref[d] + (ends[-1] if d else 0))
@@ -63,14 +69,14 @@
             seen = (key_pos >= start) & (key_pos <= pos)
             bias_ref[:, c * ROWS : (c + 1) * ROWS] = jnp.where(seen, 0.0, NEG)
 
-    first = jnp.int32(0)
+    oldest = jnp.int32(0)
     for end in ends:
-        first = jnp.where(run * ROWS >= end, end, first)
-    live = run - first // ROWS + 1
+        oldest = jnp.where(run * ROWS >= end, end, oldest)
+    live = run - oldest // ROWS + 1
 
     def work(n):
-        k = stack([r[...] for r in k_refs[:n]])
-        v = stack([r[...] for r in v_refs[:n]])
+        k = stack([r[:, at(skip + head)] for r in kv_refs[:n]])
+        v = stack([r[:, at(width + skip + head)] for r in kv_refs[:n]])
         v_one = jnp.concatenate([v, jnp.ones((n * ROWS, HD), jnp.bfloat16)], axis=1)
         bias = stack([bias_ref[:, : n * ROWS]] * HEADS_AT_ONCE)
         blocks = range(GROUP // HEADS_AT_ONCE)
@@ -107,32 +113,32 @@
         dv = dot(stack(g_scaled), stack(weights), TN)
         for c in range(n):
             cols = slice(c * ROWS, (c + 1) * ROWS)
-            part_refs[c][0, 0] = dk[:, cols].astype(jnp.bfloat16)
-            part_refs[c][0, 1] = dv[:, cols].astype(jnp.bfloat16)
+            part_refs[c][head, 0] = dk[:, cols].astype(jnp.bfloat16)
+            part_refs[c][head, 1] = dv[:, cols].astype(jnp.bfloat16)
         for c in range(n, chunks):
-            part_refs[c][...] = jnp.zeros_like(part_refs[c])
+            part_refs[c][head] = jnp.zeros_like(part_refs[c][head])
 
     sizes = [n for n in SIZES if n < chunks] + [chunks]
     for low, n in zip([0] + sizes, sizes):
         pl.when((live > low) & (live <= n))(functools.partial(work, n))
 
 
-def total(chunks, *refs):
-    part_refs, o_refs = refs[:chunks], refs[-2:]
+def total(count, *refs):
+    part_refs, o_refs = refs[:count], refs[-2:]
     for i, o_ref in enumerate(o_refs):
-        s = part_refs[0][0, i].astype(jnp.float32)
-        for r in part_refs[1:]:
-            s = s + r[0, i].astype(jnp.float32)
-        o_ref[...] = s.T.astype(jnp.bfloat16)
+        for h in range(part_refs[0].shape[0]):
+            s = part_refs[0][h, i].astype(jnp.float32)
+            for r in part_refs[1:]:
+                s = s + r[h, i].astype(jnp.float32)
+            o_ref[:, h * HD : (h + 1) * HD] = s.T.astype(jnp.bfloat16)
 
 
 def total_heads(first, count, parts, before):
-    part = pl.BlockSpec((1, 2, HD, ROWS), lambda h: (h, 0, 0, 0))
-    out = pl.BlockSpec((ROWS, HD), lambda h: (0, first + h))
+    out = pl.BlockSpec((ROWS, count * HD), lambda _: (0, first // count))
     return pl.pallas_call(
         functools.partial(total, len(parts)),
-        grid=(count,),
-        in_specs=[part] * len(parts)
+        grid=(1,),
+        in_specs=[pl.BlockSpec(memory_space=pltpu.VMEM)] * len(parts)
         + [pl.BlockSpec(memory_space=pl.ANY)] * len(before),
         out_specs=[out, out],
         out_shape=[jax.ShapeDtypeStruct((ROWS, KVH * HD), jnp.bfloat16)] * 2,
@@ -142,45 +148,38 @@
             bytes_accessed=count * 12 * HD * ROWS * 2,
             transcendentals=0,
         ),
+        compiler_params=pltpu.CompilerParams(vmem_limit_bytes=VMEM_LIMIT),
         name="total",
     )(*parts, *before)
 
 
-def attend_heads(first, count, held, lens, run, wide_args, keys, values, got, before):
-    chunks = len(got) + 1
-    flops = 12 * count * GROUP * ROWS * HD * chunks * ROWS
+def attend_heads(first, count, held, lens, run, wide_args, got, before):
+    chunks = len(got)
+    vmem = pl.BlockSpec(memory_space=pltpu.VMEM)
     wide = pl.BlockSpec((ROWS, GROUP * HD), lambda h, *_: (0, first + h))
-    own = pl.BlockSpec((ROWS, HD), lambda h, *_: (0, first + h))
-    skip, width = held
-    k_spec = pl.BlockSpec((ROWS, HD), lambda h, *_: (0, skip + h))
-    v_spec = pl.BlockSpec((ROWS, HD), lambda h, *_: (0, width + skip + h))
-    part = pl.BlockSpec((1, 2, HD, ROWS), lambda h, *_: (h, 0, 0, 0))
     part_shape = jax.ShapeDtypeStruct((count, 2, HD, ROWS), jnp.bfloat16)
     big = jax.ShapeDtypeStruct((ROWS, H * HD), jnp.bfloat16)
-    back = chunks - 1
     return pl.pallas_call(
-        functools.partial(attend, chunks, len(before)),
+        functools.partial(attend, chunks, len(before), held),
         grid_spec=pltpu.PrefetchScalarGridSpec(
             num_scalar_prefetch=2,
             grid=(count,),
             in_specs=[wide, wide]
             + [pl.BlockSpec(memory_space=pl.ANY)] * len(before)
-            + [own]
-            + [k_spec] * back
-            + [own]
-            + [v_spec] * back,
-            out_specs=[wide, wide] + [part] * chunks,
+            + [vmem] * chunks,
+            out_specs=[wide, wide] + [vmem] * chunks,
             scratch_shapes=[pltpu.VMEM((ROWS, chunks * ROWS), jnp.float32)],
         ),
         out_shape=[big, big] + [part_shape] * chunks,
         input_output_aliases={4 + i: i for i in range(len(before))},
         cost_estimate=pl.CostEstimate(
-            flops=flops,
+            flops=12 * count * GROUP * ROWS * HD * chunks * ROWS,
             bytes_accessed=4 * count * GROUP * ROWS * HD * 2,
             transcendentals=count * GROUP * ROWS * chunks * ROWS,
         ),
+        compiler_params=pltpu.CompilerParams(vmem_limit_bytes=VMEM_LIMIT),
         name="attend",
-    )(lens, run, *wide_args, *before, keys, *got, values, *got)
+    )(lens, run, *wide_args, *before, *got)
 
 
 def shift(x, by, n):
@@ -193,30 +192,20 @@
     back = min(n - 1, -(-(MOST - 1) // ROWS))
     chunks = back + 1
     run = lax.axis_index("seq").astype(jnp.int32)[None]
-    shifts = list(range(back, 0, -1))
     got = {}
-    for first in range(0, KVH, KVH // IN_PIECES):
-        count = KVH // IN_PIECES
+    count = KVH // IN_PIECES
+    for first in range(0, KVH, count):
         cols = slice(first * HD, (first + count) * HD)
         both = jnp.concatenate([keys[:, cols], values[:, cols]], axis=1)
-        here = {c: shift(both, c, n) for c in shifts}
+        here = [shift(both, c, n) for c in range(1, chunks)]
         for h in range(first, first + count):
-            got[h] = (h - first, count), [here[c] for c in range(1, chunks)]
+            got[h] = (h - first, count), [both] + here
     before, sums = (), ()
     for first in range(0, KVH, KVH // PIECES):
         count = KVH // PIECES
-        held, from_left = got[first]
+        held, runs = got[first]
         att, dq, *own = attend_heads(
-            first,
-            count,
-            held,
-            lengths[0],
-            run,
-            (queries, out_grad),
-            keys,
-            values,
-            from_left,
-            before,
+            first, count, held, lengths[0], run, (queries, out_grad), runs, before
         )
         before = att, dq
         sent = [shift(own[c], -c, n) for c in range(1, chunks)]

time: 63.9 us -> 59.8 us (0.936)
  the two profiles are of different devices: /device:TPU:322 before, /device:TPU:450 now
where the time goes in v3:
time: 59.8 us; the launch traced here: 59.3 us
  starting transfers between devices  36.4 us (61%)
  waiting for transfers between devices  9.89 us (17%)
  Pallas kernels  9.12 us (15%)
  local copies, waits for them, and re-layouts  2.91 us (5%)
  between operations  0.9 us (2%)
    ppermute x16, starting transfers between devices, shift(): return lax.ppermute(x, 'seq', pairs)  36.4 us
    ppermute x16, waiting for transfers between devices, shift(): return lax.ppermute(x, 'seq', pairs)  9.89 us
    pallas_call x2, Pallas kernels, attend_heads(): pl.pallas_call(functools.partial(attend, chunks, len(before), held), grid...  7.51 us
    unnamed x6, local copies, waits for them, and re-layouts  1.87 us
    pallas_call x2, Pallas kernels, total_heads(): pl.pallas_call(functools.partial(total, len(parts)), grid=(1,), in_specs=...  1.61 us
  transfers between devices with their start and end apart: 16, of which 3 were waited for; matrix products, arithmetic and copies ran while one was open for 0% of the time, Pallas kernels for 14%

profile of v3, /device:TPU:450, one launch (start us, length us, event | category | flops | bytes accessed | tf_op | source)
XLA Modules:
  0.0 59.3 jit_solution(11730405885269229727)
XLA Ops:
  0.6 0.0 copy-start
  0.6 1.0 %fusion = (bf16[128,256]{1,0:T(8,128)(2,1)S(1)}, bf16[128,256]{1,0:T(8,128)(2,1)S(1)}, bf16[128,256]{1,0:T(8,128)(2,1)S(1)}, bf16[128,256]{1,0:T(8,128)(2,1)S(1)}) fusion(bf16[128,512]{1,0:T(8,128)(2,1)} %param.6, bf16[128,512]{1,0:T(8,128)(2,1)} %param.7), kind=kLoop, calls=%fused_computation.2 | loop fusion | bytes 524288 | tf_op jit(solution)/shard_map/slice | solution.py:199
  1.7 3.5 %collective-permute-start = (bf16[128,512]{1,0:T(8,128)(2,1)S(1)}, bf16[128,512]{1,0:T(8,128)(2,1)S(1)}, u32[]{:S(2)}, u32[]{:S(2)}) collective-permute-start(bf16[128,512]{1,0:T(8,128)(2,1)S(1)} %pad_maximum_fusion.refs_0_), channel_id=1, source_target_pairs={{0,1},{1,2},{2,3},{3,4},{4,5},{5,6},{6,7},{8,9},{9,10},{10,11},{11... | collective-permute-start | bytes 393224 | tf_op jit(solution)/shard_map/ppermute | solution.py:187
  5.2 3.4 %collective-permute-start.1 = (bf16[128,512]{1,0:T(8,128)(2,1)S(1)}, bf16[128,512]{1,0:T(8,128)(2,1)S(1)}, u32[]{:S(2)}, u32[]{:S(2)}) collective-permute-start(bf16[128,512]{1,0:T(8,128)(2,1)S(1)} %pad_maximum_fusion.refs_0_), channel_id=1, source_target_pairs={{0,2},{1,3},{2,4},{3,5},{4,6},{5,7},{8,10},{9,11},{10,12},{11,13},... | collective-permute-start | bytes 393224 | tf_op jit(solution)/shard_map/ppermute | solution.py:187
  8.6 2.4 %collective-permute-start.2 = (bf16[128,512]{1,0:T(8,128)(2,1)S(1)}, bf16[128,512]{1,0:T(8,128)(2,1)S(1)}, u32[]{:S(2)}, u32[]{:S(2)}) collective-permute-start(bf16[128,512]{1,0:T(8,128)(2,1)S(1)} %pad_maximum_fusion.refs_0_), channel_id=1, source_target_pairs={{0,3},{1,4},{2,5},{3,6},{4,7},{8,11},{9,12},{10,13},{11,14},{12,15... | collective-permute-start | bytes 393224 | tf_op jit(solution)/shard_map/ppermute | solution.py:187
  11.1 1.3 %collective-permute-start.3 = (bf16[128,512]{1,0:T(8,128)(2,1)S(1)}, bf16[128,512]{1,0:T(8,128)(2,1)S(1)}, u32[]{:S(2)}, u32[]{:S(2)}) collective-permute-start(bf16[128,512]{1,0:T(8,128)(2,1)S(1)} %pad_maximum_fusion.refs_0_), channel_id=1, source_target_pairs={{0,4},{1,5},{2,6},{3,7},{8,12},{9,13},{10,14},{11,15},{16,20},{17,... | collective-permute-start | bytes 393224 | tf_op jit(solution)/shard_map/ppermute | solution.py:187
  12.4 2.9 %collective-permute-start.4 = (bf16[128,512]{1,0:T(8,128)(2,1)S(1)}, bf16[128,512]{1,0:T(8,128)(2,1)S(1)}, u32[]{:S(2)}, u32[]{:S(2)}) collective-permute-start(bf16[128,512]{1,0:T(8,128)(2,1)S(1)} %pad_maximum_fusion.1.refs_2_), channel_id=1, source_target_pairs={{0,1},{1,2},{2,3},{3,4},{4,5},{5,6},{6,7},{8,9},{9,10},{10,11},{11... | collective-permute-start | bytes 393224 | tf_op jit(solution)/shard_map/ppermute | solution.py:187
  15.2 0.0 collective-permute-done.refs_1_
  15.3 1.9 %collective-permute-start.5 = (bf16[128,512]{1,0:T(8,128)(2,1)S(1)}, bf16[128,512]{1,0:T(8,128)(2,1)S(1)}, u32[]{:S(2)}, u32[]{:S(2)}) collective-permute-start(bf16[128,512]{1,0:T(8,128)(2,1)S(1)} %pad_maximum_fusion.1.refs_2_), channel_id=1, source_target_pairs={{0,2},{1,3},{2,4},{3,5},{4,6},{5,7},{8,10},{9,11},{10,12},{11,13},... | collective-permute-start | bytes 393224 | tf_op jit(solution)/shard_map/ppermute | solution.py:187
  17.2 0.0 collective-permute-done.1.refs_2_
  17.2 1.3 %collective-permute-start.6 = (bf16[128,512]{1,0:T(8,128)(2,1)S(1)}, bf16[128,512]{1,0:T(8,128)(2,1)S(1)}, u32[]{:S(2)}, u32[]{:S(2)}) collective-permute-start(bf16[128,512]{1,0:T(8,128)(2,1)S(1)} %pad_maximum_fusion.1.refs_2_), channel_id=1, source_target_pairs={{0,3},{1,4},{2,5},{3,6},{4,7},{8,11},{9,12},{10,13},{11,14},{12,15... | collective-permute-start | bytes 393224 | tf_op jit(solution)/shard_map/ppermute | solution.py:187
  18.5 0.0 collective-permute-done.2.refs_3_
  18.5 3.4 %collective-permute-start.7 = (bf16[128,512]{1,0:T(8,128)(2,1)S(1)}, bf16[128,512]{1,0:T(8,128)(2,1)S(1)}, u32[]{:S(2)}, u32[]{:S(2)}) collective-permute-start(bf16[128,512]{1,0:T(8,128)(2,1)S(1)} %pad_maximum_fusion.1.refs_2_), channel_id=1, source_target_pairs={{0,4},{1,5},{2,6},{3,7},{8,12},{9,13},{10,14},{11,15},{16,20},{17,... | collective-permute-start | bytes 393224 | tf_op jit(solution)/shard_map/ppermute | solution.py:187
  21.9 0.0 collective-permute-done.3.refs_4_
  21.9 0.0 copy-start.2
  22.0 0.0 copy-done
  22.0 0.6 %copy-done.2 = s32[1,16]{1,0:T(1,128)S(1)} copy-done((s32[1,16]{1,0:T(1,128)S(1)}, s32[1,16]{1,0:T(1,128)}, u32[]{:S(2)}) %copy-start.2) | copy-done | bytes 88
  22.6 0.0 copy-start.1
  22.6 1.2 %copy-done.1 = bf16[128,4096]{1,0:T(8,128)(2,1)S(1)} copy-done((bf16[128,4096]{1,0:T(8,128)(2,1)S(1)}, bf16[128,4096]{1,0:T(8,128)(2,1)}, u32[]{:S(2)}) %copy-start.1) | copy-done | bytes 1048600
  23.8 3.7 %attend.2 = (bf16[128,4096]{1,0:T(8,128)(2,1)}, bf16[128,4096]{1,0:T(8,128)(2,1)}, bf16[2,2,128,128]{3,2,1,0:T(8,128)(2,1)S(1)}, bf16[2,2,128,128]{3,2,1,0:T(8,1...) custom-call(s32[16]{0:T(128)S(1)} %bitcast.2, ...), custom_call_target="tpu_custom_call" | custom-call | flops 2013265920 | bytes 2097152 | tf_op jit(solution)/shard_map/attend/pallas_call | solution.py:162
  27.6 3.1 %collective-permute-start.12 = (bf16[2,2,128,128]{3,2,1,0:T(8,128)(2,1)S(1)}, bf16[2,2,128,128]{3,2,1,0:T(8,128)(2,1)S(1)}, u32[]{:S(2)}, u32[]{:S(2)}) collective-permute-start(bf16[2,2,128,128]{3,2,1,0:T(8,128)(2,1)S(1)} %get-tuple-element.32), channel_id=1, source_target_pairs={{1,0},{2,1},{3,2},{4,3},{5,4},{6,5},{7,6},{9,8},{10,9},{11,10},{12... | collective-permute-start | bytes 393224 | tf_op jit(solution)/shard_map/ppermute | solution.py:187
  30.7 0.0 collective-permute-done.4.refs_3_
  30.7 2.6 %collective-permute-start.13 = (bf16[2,2,128,128]{3,2,1,0:T(8,128)(2,1)S(1)}, bf16[2,2,128,128]{3,2,1,0:T(8,128)(2,1)S(1)}, u32[]{:S(2)}, u32[]{:S(2)}) collective-permute-start(bf16[2,2,128,128]{3,2,1,0:T(8,128)(2,1)S(1)} %get-tuple-element.33), channel_id=1, source_target_pairs={{2,0},{3,1},{4,2},{5,3},{6,4},{7,5},{10,8},{11,9},{12,10},{13,11},... | collective-permute-start | bytes 393224 | tf_op jit(solution)/shard_map/ppermute | solution.py:187
  33.3 0.0 collective-permute-done.5.refs_4_
  33.3 1.3 %collective-permute-start.14 = (bf16[2,2,128,128]{3,2,1,0:T(8,128)(2,1)S(1)}, bf16[2,2,128,128]{3,2,1,0:T(8,128)(2,1)S(1)}, u32[]{:S(2)}, u32[]{:S(2)}) collective-permute-start(bf16[2,2,128,128]{3,2,1,0:T(8,128)(2,1)S(1)} %get-tuple-element.34), channel_id=1, source_target_pairs={{3,0},{4,1},{5,2},{6,3},{7,4},{11,8},{12,9},{13,10},{14,11},{15,12... | collective-permute-start | bytes 393224 | tf_op jit(solution)/shard_map/ppermute | solution.py:187
  34.6 0.0 collective-permute-done.6.refs_5_
  34.6 1.5 %collective-permute-start.15 = (bf16[2,2,128,128]{3,2,1,0:T(8,128)(2,1)S(1)}, bf16[2,2,128,128]{3,2,1,0:T(8,128)(2,1)S(1)}, u32[]{:S(2)}, u32[]{:S(2)}) collective-permute-start(bf16[2,2,128,128]{3,2,1,0:T(8,128)(2,1)S(1)} %get-tuple-element.35), channel_id=1, source_target_pairs={{4,0},{5,1},{6,2},{7,3},{12,8},{13,9},{14,10},{15,11},{20,16},{21,... | collective-permute-start | bytes 393224 | tf_op jit(solution)/shard_map/ppermute | solution.py:187
  36.1 0.0 collective-permute-done.7.refs_6_
  36.1 3.8 %attend.3 = (bf16[128,4096]{1,0:T(8,128)(2,1)}, bf16[128,4096]{1,0:T(8,128)(2,1)}, bf16[2,2,128,128]{3,2,1,0:T(8,128)(2,1)S(1)}, bf16[2,2,128,128]{3,2,1,0:T(8,1...) custom-call(s32[16]{0:T(128)S(1)} %bitcast.3, ...), custom_call_target="tpu_custom_call", output_to_operand_aliasing={{0}: (4, {}), {1}: (5, {})} | custom-call | flops 2013265920 | bytes 2097152 | tf_op jit(solution)/shard_map/attend/pallas_call | solution.py:162
  39.8 1.3 %collective-permute-start.10 = (bf16[2,2,128,128]{3,2,1,0:T(8,128)(2,1)S(1)}, bf16[2,2,128,128]{3,2,1,0:T(8,128)(2,1)S(1)}, u32[]{:S(2)}, u32[]{:S(2)}) collective-permute-start(bf16[2,2,128,128]{3,2,1,0:T(8,128)(2,1)S(1)} %get-tuple-element.29), channel_id=1, source_target_pairs={{3,0},{4,1},{5,2},{6,3},{7,4},{11,8},{12,9},{13,10},{14,11},{15,12... | collective-permute-start | bytes 393224 | tf_op jit(solution)/shard_map/ppermute | solution.py:187
  41.1 0.0 collective-permute-done.12.refs_1_
  41.1 1.3 %collective-permute-start.11 = (bf16[2,2,128,128]{3,2,1,0:T(8,128)(2,1)S(1)}, bf16[2,2,128,128]{3,2,1,0:T(8,128)(2,1)S(1)}, u32[]{:S(2)}, u32[]{:S(2)}) collective-permute-start(bf16[2,2,128,128]{3,2,1,0:T(8,128)(2,1)S(1)} %get-tuple-element.30), channel_id=1, source_target_pairs={{4,0},{5,1},{6,2},{7,3},{12,8},{13,9},{14,10},{15,11},{20,16},{21,... | collective-permute-start | bytes 393224 | tf_op jit(solution)/shard_map/ppermute | solution.py:187
  42.4 0.0 collective-permute-done.13.refs_2_
  42.4 3.4 %collective-permute-start.8 = (bf16[2,2,128,128]{3,2,1,0:T(8,128)(2,1)S(1)}, bf16[2,2,128,128]{3,2,1,0:T(8,128)(2,1)S(1)}, u32[]{:S(2)}, u32[]{:S(2)}) collective-permute-start(bf16[2,2,128,128]{3,2,1,0:T(8,128)(2,1)S(1)} %get-tuple-element.27), channel_id=1, source_target_pairs={{1,0},{2,1},{3,2},{4,3},{5,4},{6,5},{7,6},{9,8},{10,9},{11,10},{12... | collective-permute-start | bytes 393224 | tf_op jit(solution)/shard_map/ppermute | solution.py:187
  45.8 0.0 collective-permute-done.14.refs_3_
  45.8 1.9 %collective-permute-start.9 = (bf16[2,2,128,128]{3,2,1,0:T(8,128)(2,1)S(1)}, bf16[2,2,128,128]{3,2,1,0:T(8,128)(2,1)S(1)}, u32[]{:S(2)}, u32[]{:S(2)}) collective-permute-start(bf16[2,2,128,128]{3,2,1,0:T(8,128)(2,1)S(1)} %get-tuple-element.28), channel_id=1, source_target_pairs={{2,0},{3,1},{4,2},{5,3},{6,4},{7,5},{10,8},{11,9},{12,10},{13,11},... | collective-permute-start | bytes 393224 | tf_op jit(solution)/shard_map/ppermute | solution.py:187
  47.8 0.0 collective-permute-done.15.refs_4_
  47.8 0.8 %total.2 = (bf16[128,512]{1,0:T(8,128)(2,1)}, bf16[128,512]{1,0:T(8,128)(2,1)}) custom-call(bf16[2,2,128,128]{3,2,1,0:T(8,128)(2,1)S(1)} %get-tuple-element.31.refs_0_, bf16[2,2,128,128]{3,2,1,0:T(8,128)(2,1)S(1)} %collective-permute-done.12.refs_1_, bf16[2,2,128,128]{3,2,1,0:T(8,128)(2,1)S(1)} %collective-permute-done.13.refs_2_, ...), custom_call_target="tpu_custom_call" | custom-call | flops 327680 | bytes 786432 | tf_op jit(solution)/shard_map/total/pallas_call | solution.py:138
  48.6 1.7 %collective-permute-done.10.refs_3_ = bf16[2,2,128,128]{3,2,1,0:T(8,128)(2,1)S(1)} collective-permute-done((bf16[2,2,128,128]{3,2,1,0:T(8,128)(2,1)S(1)}, bf16[2,2,128,128]{3,2,1,0:T(8,128)(2,1)S(1)}, u32[]{:S(2)}, u32[]{:S(2)}) %collective-permute-start.10) | collective-permute-done | bytes 131104 | tf_op jit(solution)/shard_map/ppermute | solution.py:187
  50.3 6.1 %collective-permute-done.11.refs_4_ = bf16[2,2,128,128]{3,2,1,0:T(8,128)(2,1)S(1)} collective-permute-done((bf16[2,2,128,128]{3,2,1,0:T(8,128)(2,1)S(1)}, bf16[2,2,128,128]{3,2,1,0:T(8,128)(2,1)S(1)}, u32[]{:S(2)}, u32[]{:S(2)}) %collective-permute-start.11) | collective-permute-done | bytes 131104 | tf_op jit(solution)/shard_map/ppermute | solution.py:187
  56.4 0.0 collective-permute-done.8.refs_1_
  56.4 2.0 %collective-permute-done.9.refs_2_ = bf16[2,2,128,128]{3,2,1,0:T(8,128)(2,1)S(1)} collective-permute-done((bf16[2,2,128,128]{3,2,1,0:T(8,128)(2,1)S(1)}, bf16[2,2,128,128]{3,2,1,0:T(8,128)(2,1)S(1)}, u32[]{:S(2)}, u32[]{:S(2)}) %collective-permute-start.9) | collective-permute-done | bytes 131104 | tf_op jit(solution)/shard_map/ppermute | solution.py:187
  58.4 0.8 %total.3 = (bf16[128,512]{1,0:T(8,128)(2,1)}, bf16[128,512]{1,0:T(8,128)(2,1)}) custom-call(bf16[2,2,128,128]{3,2,1,0:T(8,128)(2,1)S(1)} %get-tuple-element.26.refs_0_, bf16[2,2,128,128]{3,2,1,0:T(8,128)(2,1)S(1)} %collective-permute-done.8.refs_1_, ...), custom_call_target="tpu_custom_call", output_to_operand_aliasing={{0}: (5, {}), {1}: (6, {})} | custom-call | flops 327680 | bytes 786432 | tf_op jit(solution)/shard_map/total/pallas_call | solution.py:138
  (2 shorter events, 0.0 us)
Async XLA Ops:
  0.6 21.3 %copy-start = (bf16[128,4096]{1,0:T(8,128)(2,1)S(1)}, bf16[128,4096]{1,0:T(8,128)(2,1)}, u32[]{:S(2)}) copy-start(bf16[128,4096]{1,0:T(8,128)(2,1)} %q_ref.3) | copy-start | bytes 3145732
  1.7 13.5 %collective-permute-start = (bf16[128,512]{1,0:T(8,128)(2,1)S(1)}, bf16[128,512]{1,0:T(8,128)(2,1)S(1)}, u32[]{:S(2)}, u32[]{:S(2)}) collective-permute-start(bf16[128,512]{1,0:T(8,128)(2,1)S(1)} %pad_maximum_fusion.refs_0_), channel_id=1, source_target_pairs={{0,1},{1,2},{2,3},{3,4},{4,5},{5,6},{6,7},{8,9},{9,10},{10,11},{11... | collective-permute-start | bytes 393224 | tf_op jit(solution)/shard_map/ppermute | solution.py:187
  5.2 12.0 %collective-permute-start.1 = (bf16[128,512]{1,0:T(8,128)(2,1)S(1)}, bf16[128,512]{1,0:T(8,128)(2,1)S(1)}, u32[]{:S(2)}, u32[]{:S(2)}) collective-permute-start(bf16[128,512]{1,0:T(8,128)(2,1)S(1)} %pad_maximum_fusion.refs_0_), channel_id=1, source_target_pairs={{0,2},{1,3},{2,4},{3,5},{4,6},{5,7},{8,10},{9,11},{10,12},{11,13},... | collective-permute-start | bytes 393224 | tf_op jit(solution)/shard_map/ppermute | solution.py:187
  8.6 9.9 %collective-permute-start.2 = (bf16[128,512]{1,0:T(8,128)(2,1)S(1)}, bf16[128,512]{1,0:T(8,128)(2,1)S(1)}, u32[]{:S(2)}, u32[]{:S(2)}) collective-permute-start(bf16[128,512]{1,0:T(8,128)(2,1)S(1)} %pad_maximum_fusion.refs_0_), channel_id=1, source_target_pairs={{0,3},{1,4},{2,5},{3,6},{4,7},{8,11},{9,12},{10,13},{11,14},{12,15... | collective-permute-start | bytes 393224 | tf_op jit(solution)/shard_map/ppermute | solution.py:187
  11.1 10.9 %collective-permute-start.3 = (bf16[128,512]{1,0:T(8,128)(2,1)S(1)}, bf16[128,512]{1,0:T(8,128)(2,1)S(1)}, u32[]{:S(2)}, u32[]{:S(2)}) collective-permute-start(bf16[128,512]{1,0:T(8,128)(2,1)S(1)} %pad_maximum_fusion.refs_0_), channel_id=1, source_target_pairs={{0,4},{1,5},{2,6},{3,7},{8,12},{9,13},{10,14},{11,15},{16,20},{17,... | collective-permute-start | bytes 393224 | tf_op jit(solution)/shard_map/ppermute | solution.py:187
  12.4 18.3 %collective-permute-start.4 = (bf16[128,512]{1,0:T(8,128)(2,1)S(1)}, bf16[128,512]{1,0:T(8,128)(2,1)S(1)}, u32[]{:S(2)}, u32[]{:S(2)}) collective-permute-start(bf16[128,512]{1,0:T(8,128)(2,1)S(1)} %pad_maximum_fusion.1.refs_2_), channel_id=1, source_target_pairs={{0,1},{1,2},{2,3},{3,4},{4,5},{5,6},{6,7},{8,9},{9,10},{10,11},{11... | collective-permute-start | bytes 393224 | tf_op jit(solution)/shard_map/ppermute | solution.py:187
  15.3 18.0 %collective-permute-start.5 = (bf16[128,512]{1,0:T(8,128)(2,1)S(1)}, bf16[128,512]{1,0:T(8,128)(2,1)S(1)}, u32[]{:S(2)}, u32[]{:S(2)}) collective-permute-start(bf16[128,512]{1,0:T(8,128)(2,1)S(1)} %pad_maximum_fusion.1.refs_2_), channel_id=1, source_target_pairs={{0,2},{1,3},{2,4},{3,5},{4,6},{5,7},{8,10},{9,11},{10,12},{11,13},... | collective-permute-start | bytes 393224 | tf_op jit(solution)/shard_map/ppermute | solution.py:187
  17.2 17.4 %collective-permute-start.6 = (bf16[128,512]{1,0:T(8,128)(2,1)S(1)}, bf16[128,512]{1,0:T(8,128)(2,1)S(1)}, u32[]{:S(2)}, u32[]{:S(2)}) collective-permute-start(bf16[128,512]{1,0:T(8,128)(2,1)S(1)} %pad_maximum_fusion.1.refs_2_), channel_id=1, source_target_pairs={{0,3},{1,4},{2,5},{3,6},{4,7},{8,11},{9,12},{10,13},{11,14},{12,15... | collective-permute-start | bytes 393224 | tf_op jit(solution)/shard_map/ppermute | solution.py:187
  18.5 17.6 %collective-permute-start.7 = (bf16[128,512]{1,0:T(8,128)(2,1)S(1)}, bf16[128,512]{1,0:T(8,128)(2,1)S(1)}, u32[]{:S(2)}, u32[]{:S(2)}) collective-permute-start(bf16[128,512]{1,0:T(8,128)(2,1)S(1)} %pad_maximum_fusion.1.refs_2_), channel_id=1, source_target_pairs={{0,4},{1,5},{2,6},{3,7},{8,12},{9,13},{10,14},{11,15},{16,20},{17,... | collective-permute-start | bytes 393224 | tf_op jit(solution)/shard_map/ppermute | solution.py:187
  21.9 0.7 %copy-start.2 = (s32[1,16]{1,0:T(1,128)S(1)}, s32[1,16]{1,0:T(1,128)}, u32[]{:S(2)}) copy-start(s32[1,16]{1,0:T(1,128)} %param.8) | copy-start | bytes 196
  22.6 1.2 %copy-start.1 = (bf16[128,4096]{1,0:T(8,128)(2,1)S(1)}, bf16[128,4096]{1,0:T(8,128)(2,1)}, u32[]{:S(2)}) copy-start(bf16[128,4096]{1,0:T(8,128)(2,1)} %g_ref.3) | copy-start | bytes 3145732
  27.6 13.6 %collective-permute-start.12 = (bf16[2,2,128,128]{3,2,1,0:T(8,128)(2,1)S(1)}, bf16[2,2,128,128]{3,2,1,0:T(8,128)(2,1)S(1)}, u32[]{:S(2)}, u32[]{:S(2)}) collective-permute-start(bf16[2,2,128,128]{3,2,1,0:T(8,128)(2,1)S(1)} %get-tuple-element.32), channel_id=1, source_target_pairs={{1,0},{2,1},{3,2},{4,3},{5,4},{6,5},{7,6},{9,8},{10,9},{11,10},{12... | collective-permute-start | bytes 393224 | tf_op jit(solution)/shard_map/ppermute | solution.py:187
  30.7 11.8 %collective-permute-start.13 = (bf16[2,2,128,128]{3,2,1,0:T(8,128)(2,1)S(1)}, bf16[2,2,128,128]{3,2,1,0:T(8,128)(2,1)S(1)}, u32[]{:S(2)}, u32[]{:S(2)}) collective-permute-start(bf16[2,2,128,128]{3,2,1,0:T(8,128)(2,1)S(1)} %get-tuple-element.33), channel_id=1, source_target_pairs={{2,0},{3,1},{4,2},{5,3},{6,4},{7,5},{10,8},{11,9},{12,10},{13,11},... | collective-permute-start | bytes 393224 | tf_op jit(solution)/shard_map/ppermute | solution.py:187
  33.3 12.6 %collective-permute-start.14 = (bf16[2,2,128,128]{3,2,1,0:T(8,128)(2,1)S(1)}, bf16[2,2,128,128]{3,2,1,0:T(8,128)(2,1)S(1)}, u32[]{:S(2)}, u32[]{:S(2)}) collective-permute-start(bf16[2,2,128,128]{3,2,1,0:T(8,128)(2,1)S(1)} %get-tuple-element.34), channel_id=1, source_target_pairs={{3,0},{4,1},{5,2},{6,3},{7,4},{11,8},{12,9},{13,10},{14,11},{15,12... | collective-permute-start | bytes 393224 | tf_op jit(solution)/shard_map/ppermute | solution.py:187
  34.6 13.2 %collective-permute-start.15 = (bf16[2,2,128,128]{3,2,1,0:T(8,128)(2,1)S(1)}, bf16[2,2,128,128]{3,2,1,0:T(8,128)(2,1)S(1)}, u32[]{:S(2)}, u32[]{:S(2)}) collective-permute-start(bf16[2,2,128,128]{3,2,1,0:T(8,128)(2,1)S(1)} %get-tuple-element.35), channel_id=1, source_target_pairs={{4,0},{5,1},{6,2},{7,3},{12,8},{13,9},{14,10},{15,11},{20,16},{21,... | collective-permute-start | bytes 393224 | tf_op jit(solution)/shard_map/ppermute | solution.py:187
  39.8 10.4 %collective-permute-start.10 = (bf16[2,2,128,128]{3,2,1,0:T(8,128)(2,1)S(1)}, bf16[2,2,128,128]{3,2,1,0:T(8,128)(2,1)S(1)}, u32[]{:S(2)}, u32[]{:S(2)}) collective-permute-start(bf16[2,2,128,128]{3,2,1,0:T(8,128)(2,1)S(1)} %get-tuple-element.29), channel_id=1, source_target_pairs={{3,0},{4,1},{5,2},{6,3},{7,4},{11,8},{12,9},{13,10},{14,11},{15,12... | collective-permute-start | bytes 393224 | tf_op jit(solution)/shard_map/ppermute | solution.py:187
  41.1 15.3 %collective-permute-start.11 = (bf16[2,2,128,128]{3,2,1,0:T(8,128)(2,1)S(1)}, bf16[2,2,128,128]{3,2,1,0:T(8,128)(2,1)S(1)}, u32[]{:S(2)}, u32[]{:S(2)}) collective-permute-start(bf16[2,2,128,128]{3,2,1,0:T(8,128)(2,1)S(1)} %get-tuple-element.30), channel_id=1, source_target_pairs={{4,0},{5,1},{6,2},{7,3},{12,8},{13,9},{14,10},{15,11},{20,16},{21,... | collective-permute-start | bytes 393224 | tf_op jit(solution)/shard_map/ppermute | solution.py:187
  42.4 14.0 %collective-permute-start.8 = (bf16[2,2,128,128]{3,2,1,0:T(8,128)(2,1)S(1)}, bf16[2,2,128,128]{3,2,1,0:T(8,128)(2,1)S(1)}, u32[]{:S(2)}, u32[]{:S(2)}) collective-permute-start(bf16[2,2,128,128]{3,2,1,0:T(8,128)(2,1)S(1)} %get-tuple-element.27), channel_id=1, source_target_pairs={{1,0},{2,1},{3,2},{4,3},{5,4},{6,5},{7,6},{9,8},{10,9},{11,10},{12... | collective-permute-start | bytes 393224 | tf_op jit(solution)/shard_map/ppermute | solution.py:187
  45.8 12.6 %collective-permute-start.9 = (bf16[2,2,128,128]{3,2,1,0:T(8,128)(2,1)S(1)}, bf16[2,2,128,128]{3,2,1,0:T(8,128)(2,1)S(1)}, u32[]{:S(2)}, u32[]{:S(2)}) collective-permute-start(bf16[2,2,128,128]{3,2,1,0:T(8,128)(2,1)S(1)} %get-tuple-element.28), channel_id=1, source_target_pairs={{2,0},{3,1},{4,2},{5,3},{6,4},{7,5},{10,8},{11,9},{12,10},{13,11},... | collective-permute-start | bytes 393224 | tf_op jit(solution)/shard_map/ppermute | solution.py:187

commit v4 on v3

--- a/solution.py
+++ b/solution.py
@@ -20,9 +20,8 @@
 ROWS = 128
 HEADS_AT_ONCE = 2
 SIZES = (1, 2, 3, 4)
-VMEM_LIMIT = 48 * 2**20
-PIECES = 2
-IN_PIECES = 2
+VMEM_LIMIT = 52 * 2**20
+PIECES = ((0, 3), (3, 1))
 
 NT = (((1,), (1,)), ((), ()))
 TN = (((0,), (0,)), ((), ()))
@@ -192,20 +191,16 @@
     back = min(n - 1, -(-(MOST - 1) // ROWS))
     chunks = back + 1
     run = lax.axis_index("seq").astype(jnp.int32)[None]
-    got = {}
-    count = KVH // IN_PIECES
-    for first in range(0, KVH, count):
+    got = []
+    for first, count in PIECES:
         cols = slice(first * HD, (first + count) * HD)
         both = jnp.concatenate([keys[:, cols], values[:, cols]], axis=1)
         here = [shift(both, c, n) for c in range(1, chunks)]
-        for h in range(first, first + count):
-            got[h] = (h - first, count), [both] + here
+        got.append([both] + here)
     before, sums = (), ()
-    for first in range(0, KVH, KVH // PIECES):
-        count = KVH // PIECES
-        held, runs = got[first]
+    for (first, count), runs in zip(PIECES, got):
         att, dq, *own = attend_heads(
-            first, count, held, lengths[0], run, (queries, out_grad), runs, before
+            first, count, (0, count), lengths[0], run, (queries, out_grad), runs, before
         )
         before = att, dq
         sent = [shift(own[c], -c, n) for c in range(1, chunks)]

time: 59.8 us -> 65.2 us (1.090)
  the two profiles are of different devices: /device:TPU:450 before, /device:TPU:380 now
where the time goes in v4:
time: 65.2 us; the launch traced here: 64.5 us
  starting transfers between devices  38.5 us (59%)
  waiting for transfers between devices  11.7 us (18%)
  Pallas kernels  11 us (17%)
  local copies, waits for them, and re-layouts  2.36 us (4%)
  between operations  0.87 us (1%)
    ppermute x16, starting transfers between devices, shift(): return lax.ppermute(x, 'seq', pairs)  38.5 us
    ppermute x16, waiting for transfers between devices, shift(): return lax.ppermute(x, 'seq', pairs)  11.7 us
    pallas_call x2, Pallas kernels, attend_heads(): pl.pallas_call(functools.partial(attend, chunks, len(before), held), grid...  9.43 us
    slice x8, local copies, waits for them, and re-layouts, shards(): both = jnp.concatenate([keys[:, cols], values[:, cols]], axis=1)  1.7 us
    pallas_call x2, Pallas kernels, total_heads(): pl.pallas_call(functools.partial(total, len(parts)), grid=(1,), in_specs=...  1.61 us
  transfers between devices with their start and end apart: 16, of which 6 were waited for; matrix products, arithmetic and copies ran while one was open for 0% of the time, Pallas kernels for 16%

profile of v4, /device:TPU:380, one launch (start us, length us, event | category | flops | bytes accessed | tf_op | source)
XLA Modules:
  0.0 64.5 jit_solution(9277785766061109114)
XLA Ops:
  0.6 0.0 slice-start
  0.6 0.0 slice-start.2
  0.7 0.9 %slice-done = bf16[128,384]{1,0:T(8,128)(2,1)S(1)} async-done(((bf16[128,512]{1,0:T(8,128)(2,1)}), bf16[128,384]{1,0:T(8,128)(2,1)S(1)}, s32[]{:S(2)}) %slice-start) | async-done | bytes 98328 | tf_op jit(solution)/shard_map/slice | solution.py:197
  1.5 0.0 slice-done.2
  1.6 3.3 %collective-permute-start = (bf16[128,768]{1,0:T(8,128)(2,1)S(1)}, bf16[128,768]{1,0:T(8,128)(2,1)S(1)}, u32[]{:S(2)}, u32[]{:S(2)}) collective-permute-start(bf16[128,768]{1,0:T(8,128)(2,1)S(1)} %pad_maximum_fusion.refs_0_), channel_id=1, source_target_pairs={{0,1},{1,2},{2,3},{3,4},{4,5},{5,6},{6,7},{8,9},{9,10},{10,11},{11... | collective-permute-start | bytes 589832 | tf_op jit(solution)/shard_map/ppermute | solution.py:186
  4.9 1.9 %collective-permute-start.1 = (bf16[128,768]{1,0:T(8,128)(2,1)S(1)}, bf16[128,768]{1,0:T(8,128)(2,1)S(1)}, u32[]{:S(2)}, u32[]{:S(2)}) collective-permute-start(bf16[128,768]{1,0:T(8,128)(2,1)S(1)} %pad_maximum_fusion.refs_0_), channel_id=1, source_target_pairs={{0,2},{1,3},{2,4},{3,5},{4,6},{5,7},{8,10},{9,11},{10,12},{11,13},... | collective-permute-start | bytes 589832 | tf_op jit(solution)/shard_map/ppermute | solution.py:186
  6.8 1.3 %collective-permute-start.2 = (bf16[128,768]{1,0:T(8,128)(2,1)S(1)}, bf16[128,768]{1,0:T(8,128)(2,1)S(1)}, u32[]{:S(2)}, u32[]{:S(2)}) collective-permute-start(bf16[128,768]{1,0:T(8,128)(2,1)S(1)} %pad_maximum_fusion.refs_0_), channel_id=1, source_target_pairs={{0,3},{1,4},{2,5},{3,6},{4,7},{8,11},{9,12},{10,13},{11,14},{12,15... | collective-permute-start | bytes 589832 | tf_op jit(solution)/shard_map/ppermute | solution.py:186
  8.1 1.3 %collective-permute-start.3 = (bf16[128,768]{1,0:T(8,128)(2,1)S(1)}, bf16[128,768]{1,0:T(8,128)(2,1)S(1)}, u32[]{:S(2)}, u32[]{:S(2)}) collective-permute-start(bf16[128,768]{1,0:T(8,128)(2,1)S(1)} %pad_maximum_fusion.refs_0_), channel_id=1, source_target_pairs={{0,4},{1,5},{2,6},{3,7},{8,12},{9,13},{10,14},{11,15},{16,20},{17,... | collective-permute-start | bytes 589832 | tf_op jit(solution)/shard_map/ppermute | solution.py:186
  9.4 0.0 slice-start.1
  9.4 0.0 slice-start.3
  9.4 0.7 %slice-done.1 = bf16[128,128]{1,0:T(8,128)(2,1)S(1)} async-done(((bf16[128,512]{1,0:T(8,128)(2,1)}), bf16[128,128]{1,0:T(8,128)(2,1)S(1)}, s32[]{:S(2)}) %slice-start.1) | async-done | bytes 32792 | tf_op jit(solution)/shard_map/slice | solution.py:197
  10.2 0.0 slice-done.3
  10.2 2.6 %collective-permute-start.4 = (bf16[128,256]{1,0:T(8,128)(2,1)S(1)}, bf16[128,256]{1,0:T(8,128)(2,1)S(1)}, u32[]{:S(2)}, u32[]{:S(2)}) collective-permute-start(bf16[128,256]{1,0:T(8,128)(2,1)S(1)} %pad_maximum_fusion.1.refs_2_), channel_id=1, source_target_pairs={{0,1},{1,2},{2,3},{3,4},{4,5},{5,6},{6,7},{8,9},{9,10},{10,11},{11... | collective-permute-start | bytes 196616 | tf_op jit(solution)/shard_map/ppermute | solution.py:186
  12.8 0.0 collective-permute-done.refs_1_
  12.8 1.9 %collective-permute-start.5 = (bf16[128,256]{1,0:T(8,128)(2,1)S(1)}, bf16[128,256]{1,0:T(8,128)(2,1)S(1)}, u32[]{:S(2)}, u32[]{:S(2)}) collective-permute-start(bf16[128,256]{1,0:T(8,128)(2,1)S(1)} %pad_maximum_fusion.1.refs_2_), channel_id=1, source_target_pairs={{0,2},{1,3},{2,4},{3,5},{4,6},{5,7},{8,10},{9,11},{10,12},{11,13},... | collective-permute-start | bytes 196616 | tf_op jit(solution)/shard_map/ppermute | solution.py:186
  14.7 0.9 %collective-permute-done.1.refs_2_ = bf16[128,768]{1,0:T(8,128)(2,1)S(1)} collective-permute-done((bf16[128,768]{1,0:T(8,128)(2,1)S(1)}, bf16[128,768]{1,0:T(8,128)(2,1)S(1)}, u32[]{:S(2)}, u32[]{:S(2)}) %collective-permute-start.1) | collective-permute-done | bytes 196640 | tf_op jit(solution)/shard_map/ppermute | solution.py:186
  15.6 1.3 %collective-permute-start.6 = (bf16[128,256]{1,0:T(8,128)(2,1)S(1)}, bf16[128,256]{1,0:T(8,128)(2,1)S(1)}, u32[]{:S(2)}, u32[]{:S(2)}) collective-permute-start(bf16[128,256]{1,0:T(8,128)(2,1)S(1)} %pad_maximum_fusion.1.refs_2_), channel_id=1, source_target_pairs={{0,3},{1,4},{2,5},{3,6},{4,7},{8,11},{9,12},{10,13},{11,14},{12,15... | collective-permute-start | bytes 196616 | tf_op jit(solution)/shard_map/ppermute | solution.py:186
  16.9 4.1 %collective-permute-done.2.refs_3_ = bf16[128,768]{1,0:T(8,128)(2,1)S(1)} collective-permute-done((bf16[128,768]{1,0:T(8,128)(2,1)S(1)}, bf16[128,768]{1,0:T(8,128)(2,1)S(1)}, u32[]{:S(2)}, u32[]{:S(2)}) %collective-permute-start.2) | collective-permute-done | bytes 196640 | tf_op jit(solution)/shard_map/ppermute | solution.py:186
  21.0 3.0 %collective-permute-done.3.refs_4_ = bf16[128,768]{1,0:T(8,128)(2,1)S(1)} collective-permute-done((bf16[128,768]{1,0:T(8,128)(2,1)S(1)}, bf16[128,768]{1,0:T(8,128)(2,1)S(1)}, u32[]{:S(2)}, u32[]{:S(2)}) %collective-permute-start.3) | collective-permute-done | bytes 196640 | tf_op jit(solution)/shard_map/ppermute | solution.py:186
  24.0 0.0 copy-start.1
  24.1 0.7 %copy-done.1 = s32[1,16]{1,0:T(1,128)S(1)} copy-done((s32[1,16]{1,0:T(1,128)S(1)}, s32[1,16]{1,0:T(1,128)}, u32[]{:S(2)}) %copy-start.1) | copy-done | bytes 88
  24.7 0.0 copy-start
  24.7 5.8 %attend.2 = (bf16[128,4096]{1,0:T(8,128)(2,1)}, bf16[128,4096]{1,0:T(8,128)(2,1)}, bf16[3,2,128,128]{3,2,1,0:T(8,128)(2,1)S(1)}, bf16[3,2,128,128]{3,2,1,0:T(8,1...) custom-call(s32[16]{0:T(128)S(1)} %bitcast.2, ...), custom_call_target="tpu_custom_call" | custom-call | flops 3019898880 | bytes 3145728 | tf_op jit(solution)/shard_map/attend/pallas_call | solution.py:161
  30.5 5.3 %collective-permute-start.12 = (bf16[3,2,128,128]{3,2,1,0:T(8,128)(2,1)S(1)}, bf16[3,2,128,128]{3,2,1,0:T(8,128)(2,1)S(1)}, u32[]{:S(2)}, u32[]{:S(2)}) collective-permute-start(bf16[3,2,128,128]{3,2,1,0:T(8,128)(2,1)S(1)} %get-tuple-element.32), channel_id=1, source_target_pairs={{1,0},{2,1},{3,2},{4,3},{5,4},{6,5},{7,6},{9,8},{10,9},{11,10},{12... | collective-permute-start | bytes 589832 | tf_op jit(solution)/shard_map/ppermute | solution.py:186
  35.9 1.9 %collective-permute-start.13 = (bf16[3,2,128,128]{3,2,1,0:T(8,128)(2,1)S(1)}, bf16[3,2,128,128]{3,2,1,0:T(8,128)(2,1)S(1)}, u32[]{:S(2)}, u32[]{:S(2)}) collective-permute-start(bf16[3,2,128,128]{3,2,1,0:T(8,128)(2,1)S(1)} %get-tuple-element.33), channel_id=1, source_target_pairs={{2,0},{3,1},{4,2},{5,3},{6,4},{7,5},{10,8},{11,9},{12,10},{13,11},... | collective-permute-start | bytes 589832 | tf_op jit(solution)/shard_map/ppermute | solution.py:186
  37.8 0.0 collective-permute-done.4.refs_3_
  37.8 1.3 %collective-permute-start.14 = (bf16[3,2,128,128]{3,2,1,0:T(8,128)(2,1)S(1)}, bf16[3,2,128,128]{3,2,1,0:T(8,128)(2,1)S(1)}, u32[]{:S(2)}, u32[]{:S(2)}) collective-permute-start(bf16[3,2,128,128]{3,2,1,0:T(8,128)(2,1)S(1)} %get-tuple-element.34), channel_id=1, source_target_pairs={{3,0},{4,1},{5,2},{6,3},{7,4},{11,8},{12,9},{13,10},{14,11},{15,12... | collective-permute-start | bytes 589832 | tf_op jit(solution)/shard_map/ppermute | solution.py:186
  39.1 0.0 collective-permute-done.5.refs_4_
  39.1 1.3 %collective-permute-start.7 = (bf16[128,256]{1,0:T(8,128)(2,1)S(1)}, bf16[128,256]{1,0:T(8,128)(2,1)S(1)}, u32[]{:S(2)}, u32[]{:S(2)}) collective-permute-start(bf16[128,256]{1,0:T(8,128)(2,1)S(1)} %pad_maximum_fusion.1.refs_2_), channel_id=1, source_target_pairs={{0,4},{1,5},{2,6},{3,7},{8,12},{9,13},{10,14},{11,15},{16,20},{17,... | collective-permute-start | bytes 196616 | tf_op jit(solution)/shard_map/ppermute | solution.py:186
  40.4 0.0 collective-permute-done.6.refs_5_
  40.5 6.1 %collective-permute-start.15 = (bf16[3,2,128,128]{3,2,1,0:T(8,128)(2,1)S(1)}, bf16[3,2,128,128]{3,2,1,0:T(8,128)(2,1)S(1)}, u32[]{:S(2)}, u32[]{:S(2)}) collective-permute-start(bf16[3,2,128,128]{3,2,1,0:T(8,128)(2,1)S(1)} %get-tuple-element.35), channel_id=1, source_target_pairs={{4,0},{5,1},{6,2},{7,3},{12,8},{13,9},{14,10},{15,11},{20,16},{21,... | collective-permute-start | bytes 589832 | tf_op jit(solution)/shard_map/ppermute | solution.py:186
  46.5 0.3 collective-permute-done.7.refs_6_
  46.8 0.0 copy-done
  46.8 3.6 %attend.3 = (bf16[128,4096]{1,0:T(8,128)(2,1)}, bf16[128,4096]{1,0:T(8,128)(2,1)}, bf16[1,2,128,128]{3,2,1,0:T(8,128)(2,1)S(1)}, bf16[1,2,128,128]{3,2,1,0:T(8,1...) custom-call(s32[16]{0:T(128)S(1)} %bitcast.3, ...), custom_call_target="tpu_custom_call", output_to_operand_aliasing={{0}: (4, {}), {1}: (5, {})} | custom-call | flops 1006632960 | bytes 1048576 | tf_op jit(solution)/shard_map/attend/pallas_call | solution.py:161
  50.4 1.5 %collective-permute-start.10 = (bf16[1,2,128,128]{3,2,1,0:T(8,128)(2,1)S(1)}, bf16[1,2,128,128]{3,2,1,0:T(8,128)(2,1)S(1)}, u32[]{:S(2)}, u32[]{:S(2)}) collective-permute-start(bf16[1,2,128,128]{3,2,1,0:T(8,128)(2,1)S(1)} %get-tuple-element.29), channel_id=1, source_target_pairs={{3,0},{4,1},{5,2},{6,3},{7,4},{11,8},{12,9},{13,10},{14,11},{15,12... | collective-permute-start | bytes 196616 | tf_op jit(solution)/shard_map/ppermute | solution.py:186
  51.9 0.0 collective-permute-done.12.refs_1_
  51.9 1.4 %collective-permute-start.11 = (bf16[1,2,128,128]{3,2,1,0:T(8,128)(2,1)S(1)}, bf16[1,2,128,128]{3,2,1,0:T(8,128)(2,1)S(1)}, u32[]{:S(2)}, u32[]{:S(2)}) collective-permute-start(bf16[1,2,128,128]{3,2,1,0:T(8,128)(2,1)S(1)} %get-tuple-element.30), channel_id=1, source_target_pairs={{4,0},{5,1},{6,2},{7,3},{12,8},{13,9},{14,10},{15,11},{20,16},{21,... | collective-permute-start | bytes 196616 | tf_op jit(solution)/shard_map/ppermute | solution.py:186
  53.3 0.0 collective-permute-done.13.refs_2_
  53.3 4.3 %collective-permute-start.8 = (bf16[1,2,128,128]{3,2,1,0:T(8,128)(2,1)S(1)}, bf16[1,2,128,128]{3,2,1,0:T(8,128)(2,1)S(1)}, u32[]{:S(2)}, u32[]{:S(2)}) collective-permute-start(bf16[1,2,128,128]{3,2,1,0:T(8,128)(2,1)S(1)} %get-tuple-element.27), channel_id=1, source_target_pairs={{1,0},{2,1},{3,2},{4,3},{5,4},{6,5},{7,6},{9,8},{10,9},{11,10},{12... | collective-permute-start | bytes 196616 | tf_op jit(solution)/shard_map/ppermute | solution.py:186
  57.6 0.0 collective-permute-done.14.refs_3_
  57.6 1.9 %collective-permute-start.9 = (bf16[1,2,128,128]{3,2,1,0:T(8,128)(2,1)S(1)}, bf16[1,2,128,128]{3,2,1,0:T(8,128)(2,1)S(1)}, u32[]{:S(2)}, u32[]{:S(2)}) collective-permute-start(bf16[1,2,128,128]{3,2,1,0:T(8,128)(2,1)S(1)} %get-tuple-element.28), channel_id=1, source_target_pairs={{2,0},{3,1},{4,2},{5,3},{6,4},{7,5},{10,8},{11,9},{12,10},{13,11},... | collective-permute-start | bytes 196616 | tf_op jit(solution)/shard_map/ppermute | solution.py:186
  59.5 0.0 collective-permute-done.15.refs_4_
  59.5 0.9 %total.2 = (bf16[128,512]{1,0:T(8,128)(2,1)}, bf16[128,512]{1,0:T(8,128)(2,1)}) custom-call(bf16[3,2,128,128]{3,2,1,0:T(8,128)(2,1)S(1)} %get-tuple-element.31.refs_0_, bf16[3,2,128,128]{3,2,1,0:T(8,128)(2,1)S(1)} %collective-permute-done.12.refs_1_, bf16[3,2,128,128]{3,2,1,0:T(8,128)(2,1)S(1)} %collective-permute-done.13.refs_2_, ...), custom_call_target="tpu_custom_call" | custom-call | flops 491520 | bytes 1179648 | tf_op jit(solution)/shard_map/total/pallas_call | solution.py:137
  60.4 0.0 collective-permute-done.10.refs_3_
  60.4 0.0 collective-permute-done.11.refs_4_
  60.4 0.8 %collective-permute-done.8.refs_1_ = bf16[1,2,128,128]{3,2,1,0:T(8,128)(2,1)S(1)} collective-permute-done((bf16[1,2,128,128]{3,2,1,0:T(8,128)(2,1)S(1)}, bf16[1,2,128,128]{3,2,1,0:T(8,128)(2,1)S(1)}, u32[]{:S(2)}, u32[]{:S(2)}) %collective-permute-start.8) | collective-permute-done | bytes 65568 | tf_op jit(solution)/shard_map/ppermute | solution.py:186
  61.2 2.5 %collective-permute-done.9.refs_2_ = bf16[1,2,128,128]{3,2,1,0:T(8,128)(2,1)S(1)} collective-permute-done((bf16[1,2,128,128]{3,2,1,0:T(8,128)(2,1)S(1)}, bf16[1,2,128,128]{3,2,1,0:T(8,128)(2,1)S(1)}, u32[]{:S(2)}, u32[]{:S(2)}) %collective-permute-start.9) | collective-permute-done | bytes 65568 | tf_op jit(solution)/shard_map/ppermute | solution.py:186
  63.7 0.7 %total.3 = (bf16[128,512]{1,0:T(8,128)(2,1)}, bf16[128,512]{1,0:T(8,128)(2,1)}) custom-call(bf16[1,2,128,128]{3,2,1,0:T(8,128)(2,1)S(1)} %get-tuple-element.26.refs_0_, bf16[1,2,128,128]{3,2,1,0:T(8,128)(2,1)S(1)} %collective-permute-done.8.refs_1_, ...), custom_call_target="tpu_custom_call", output_to_operand_aliasing={{0}: (5, {}), {1}: (6, {})} | custom-call | flops 163840 | bytes 393216 | tf_op jit(solution)/shard_map/total/pallas_call | solution.py:137
  (2 shorter events, 0.0 us)
Async XLA Ops:
  0.6 0.9 %slice-start = ((bf16[128,512]{1,0:T(8,128)(2,1)}), bf16[128,384]{1,0:T(8,128)(2,1)S(1)}, s32[]{:S(2)}) async-start(bf16[128,512]{1,0:T(8,128)(2,1)} %param.6), calls=%async_computation | async-start | bytes 196608 | tf_op jit(solution)/shard_map/slice | solution.py:197
  0.6 0.9 %slice-start.2 = ((bf16[128,512]{1,0:T(8,128)(2,1)}), bf16[128,384]{1,0:T(8,128)(2,1)S(1)}, s32[]{:S(2)}) async-start(bf16[128,512]{1,0:T(8,128)(2,1)} %param.7), calls=%async_computation.2 | async-start | bytes 196608 | tf_op jit(solution)/shard_map/slice | solution.py:197
  1.6 11.2 %collective-permute-start = (bf16[128,768]{1,0:T(8,128)(2,1)S(1)}, bf16[128,768]{1,0:T(8,128)(2,1)S(1)}, u32[]{:S(2)}, u32[]{:S(2)}) collective-permute-start(bf16[128,768]{1,0:T(8,128)(2,1)S(1)} %pad_maximum_fusion.refs_0_), channel_id=1, source_target_pairs={{0,1},{1,2},{2,3},{3,4},{4,5},{5,6},{6,7},{8,9},{9,10},{10,11},{11... | collective-permute-start | bytes 589832 | tf_op jit(solution)/shard_map/ppermute | solution.py:186
  4.9 10.7 %collective-permute-start.1 = (bf16[128,768]{1,0:T(8,128)(2,1)S(1)}, bf16[128,768]{1,0:T(8,128)(2,1)S(1)}, u32[]{:S(2)}, u32[]{:S(2)}) collective-permute-start(bf16[128,768]{1,0:T(8,128)(2,1)S(1)} %pad_maximum_fusion.refs_0_), channel_id=1, source_target_pairs={{0,2},{1,3},{2,4},{3,5},{4,6},{5,7},{8,10},{9,11},{10,12},{11,13},... | collective-permute-start | bytes 589832 | tf_op jit(solution)/shard_map/ppermute | solution.py:186
  6.8 14.2 %collective-permute-start.2 = (bf16[128,768]{1,0:T(8,128)(2,1)S(1)}, bf16[128,768]{1,0:T(8,128)(2,1)S(1)}, u32[]{:S(2)}, u32[]{:S(2)}) collective-permute-start(bf16[128,768]{1,0:T(8,128)(2,1)S(1)} %pad_maximum_fusion.refs_0_), channel_id=1, source_target_pairs={{0,3},{1,4},{2,5},{3,6},{4,7},{8,11},{9,12},{10,13},{11,14},{12,15... | collective-permute-start | bytes 589832 | tf_op jit(solution)/shard_map/ppermute | solution.py:186
  8.1 15.9 %collective-permute-start.3 = (bf16[128,768]{1,0:T(8,128)(2,1)S(1)}, bf16[128,768]{1,0:T(8,128)(2,1)S(1)}, u32[]{:S(2)}, u32[]{:S(2)}) collective-permute-start(bf16[128,768]{1,0:T(8,128)(2,1)S(1)} %pad_maximum_fusion.refs_0_), channel_id=1, source_target_pairs={{0,4},{1,5},{2,6},{3,7},{8,12},{9,13},{10,14},{11,15},{16,20},{17,... | collective-permute-start | bytes 589832 | tf_op jit(solution)/shard_map/ppermute | solution.py:186
  9.4 0.8 %slice-start.1 = ((bf16[128,512]{1,0:T(8,128)(2,1)}), bf16[128,128]{1,0:T(8,128)(2,1)S(1)}, s32[]{:S(2)}) async-start(bf16[128,512]{1,0:T(8,128)(2,1)} %param.6), calls=%async_computation.1 | async-start | bytes 65536 | tf_op jit(solution)/shard_map/slice | solution.py:197
  9.4 0.8 %slice-start.3 = ((bf16[128,512]{1,0:T(8,128)(2,1)}), bf16[128,128]{1,0:T(8,128)(2,1)S(1)}, s32[]{:S(2)}) async-start(bf16[128,512]{1,0:T(8,128)(2,1)} %param.7), calls=%async_computation.3 | async-start | bytes 65536 | tf_op jit(solution)/shard_map/slice | solution.py:197
  10.2 27.6 %collective-permute-start.4 = (bf16[128,256]{1,0:T(8,128)(2,1)S(1)}, bf16[128,256]{1,0:T(8,128)(2,1)S(1)}, u32[]{:S(2)}, u32[]{:S(2)}) collective-permute-start(bf16[128,256]{1,0:T(8,128)(2,1)S(1)} %pad_maximum_fusion.1.refs_2_), channel_id=1, source_target_pairs={{0,1},{1,2},{2,3},{3,4},{4,5},{5,6},{6,7},{8,9},{9,10},{10,11},{11... | collective-permute-start | bytes 196616 | tf_op jit(solution)/shard_map/ppermute | solution.py:186
  12.8 26.3 %collective-permute-start.5 = (bf16[128,256]{1,0:T(8,128)(2,1)S(1)}, bf16[128,256]{1,0:T(8,128)(2,1)S(1)}, u32[]{:S(2)}, u32[]{:S(2)}) collective-permute-start(bf16[128,256]{1,0:T(8,128)(2,1)S(1)} %pad_maximum_fusion.1.refs_2_), channel_id=1, source_target_pairs={{0,2},{1,3},{2,4},{3,5},{4,6},{5,7},{8,10},{9,11},{10,12},{11,13},... | collective-permute-start | bytes 196616 | tf_op jit(solution)/shard_map/ppermute | solution.py:186
  15.6 24.8 %collective-permute-start.6 = (bf16[128,256]{1,0:T(8,128)(2,1)S(1)}, bf16[128,256]{1,0:T(8,128)(2,1)S(1)}, u32[]{:S(2)}, u32[]{:S(2)}) collective-permute-start(bf16[128,256]{1,0:T(8,128)(2,1)S(1)} %pad_maximum_fusion.1.refs_2_), channel_id=1, source_target_pairs={{0,3},{1,4},{2,5},{3,6},{4,7},{8,11},{9,12},{10,13},{11,14},{12,15... | collective-permute-start | bytes 196616 | tf_op jit(solution)/shard_map/ppermute | solution.py:186
  24.0 0.7 %copy-start.1 = (s32[1,16]{1,0:T(1,128)S(1)}, s32[1,16]{1,0:T(1,128)}, u32[]{:S(2)}) copy-start(s32[1,16]{1,0:T(1,128)} %param.8) | copy-start | bytes 196
  24.7 22.1 %copy-start = (bf16[128,4096]{1,0:T(8,128)(2,1)S(1)}, bf16[128,4096]{1,0:T(8,128)(2,1)}, u32[]{:S(2)}) copy-start(bf16[128,4096]{1,0:T(8,128)(2,1)} %q_ref.3) | copy-start | bytes 3145732
  30.5 21.4 %collective-permute-start.12 = (bf16[3,2,128,128]{3,2,1,0:T(8,128)(2,1)S(1)}, bf16[3,2,128,128]{3,2,1,0:T(8,128)(2,1)S(1)}, u32[]{:S(2)}, u32[]{:S(2)}) collective-permute-start(bf16[3,2,128,128]{3,2,1,0:T(8,128)(2,1)S(1)} %get-tuple-element.32), channel_id=1, source_target_pairs={{1,0},{2,1},{3,2},{4,3},{5,4},{6,5},{7,6},{9,8},{10,9},{11,10},{12... | collective-permute-start | bytes 589832 | tf_op jit(solution)/shard_map/ppermute | solution.py:186
  35.9 17.4 %collective-permute-start.13 = (bf16[3,2,128,128]{3,2,1,0:T(8,128)(2,1)S(1)}, bf16[3,2,128,128]{3,2,1,0:T(8,128)(2,1)S(1)}, u32[]{:S(2)}, u32[]{:S(2)}) collective-permute-start(bf16[3,2,128,128]{3,2,1,0:T(8,128)(2,1)S(1)} %get-tuple-element.33), channel_id=1, source_target_pairs={{2,0},{3,1},{4,2},{5,3},{6,4},{7,5},{10,8},{11,9},{12,10},{13,11},... | collective-permute-start | bytes 589832 | tf_op jit(solution)/shard_map/ppermute | solution.py:186
  37.8 19.8 %collective-permute-start.14 = (bf16[3,2,128,128]{3,2,1,0:T(8,128)(2,1)S(1)}, bf16[3,2,128,128]{3,2,1,0:T(8,128)(2,1)S(1)}, u32[]{:S(2)}, u32[]{:S(2)}) collective-permute-start(bf16[3,2,128,128]{3,2,1,0:T(8,128)(2,1)S(1)} %get-tuple-element.34), channel_id=1, source_target_pairs={{3,0},{4,1},{5,2},{6,3},{7,4},{11,8},{12,9},{13,10},{14,11},{15,12... | collective-permute-start | bytes 589832 | tf_op jit(solution)/shard_map/ppermute | solution.py:186
  39.1 7.7 %collective-permute-start.7 = (bf16[128,256]{1,0:T(8,128)(2,1)S(1)}, bf16[128,256]{1,0:T(8,128)(2,1)S(1)}, u32[]{:S(2)}, u32[]{:S(2)}) collective-permute-start(bf16[128,256]{1,0:T(8,128)(2,1)S(1)} %pad_maximum_fusion.1.refs_2_), channel_id=1, source_target_pairs={{0,4},{1,5},{2,6},{3,7},{8,12},{9,13},{10,14},{11,15},{16,20},{17,... | collective-permute-start | bytes 196616 | tf_op jit(solution)/shard_map/ppermute | solution.py:186
  40.5 19.1 %collective-permute-start.15 = (bf16[3,2,128,128]{3,2,1,0:T(8,128)(2,1)S(1)}, bf16[3,2,128,128]{3,2,1,0:T(8,128)(2,1)S(1)}, u32[]{:S(2)}, u32[]{:S(2)}) collective-permute-start(bf16[3,2,128,128]{3,2,1,0:T(8,128)(2,1)S(1)} %get-tuple-element.35), channel_id=1, source_target_pairs={{4,0},{5,1},{6,2},{7,3},{12,8},{13,9},{14,10},{15,11},{20,16},{21,... | collective-permute-start | bytes 589832 | tf_op jit(solution)/shard_map/ppermute | solution.py:186
  50.4 10.0 %collective-permute-start.10 = (bf16[1,2,128,128]{3,2,1,0:T(8,128)(2,1)S(1)}, bf16[1,2,128,128]{3,2,1,0:T(8,128)(2,1)S(1)}, u32[]{:S(2)}, u32[]{:S(2)}) collective-permute-start(bf16[1,2,128,128]{3,2,1,0:T(8,128)(2,1)S(1)} %get-tuple-element.29), channel_id=1, source_target_pairs={{3,0},{4,1},{5,2},{6,3},{7,4},{11,8},{12,9},{13,10},{14,11},{15,12... | collective-permute-start | bytes 196616 | tf_op jit(solution)/shard_map/ppermute | solution.py:186
  51.9 8.5 %collective-permute-start.11 = (bf16[1,2,128,128]{3,2,1,0:T(8,128)(2,1)S(1)}, bf16[1,2,128,128]{3,2,1,0:T(8,128)(2,1)S(1)}, u32[]{:S(2)}, u32[]{:S(2)}) collective-permute-start(bf16[1,2,128,128]{3,2,1,0:T(8,128)(2,1)S(1)} %get-tuple-element.30), channel_id=1, source_target_pairs={{4,0},{5,1},{6,2},{7,3},{12,8},{13,9},{14,10},{15,11},{20,16},{21,... | collective-permute-start | bytes 196616 | tf_op jit(solution)/shard_map/ppermute | solution.py:186
  53.3 7.9 %collective-permute-start.8 = (bf16[1,2,128,128]{3,2,1,0:T(8,128)(2,1)S(1)}, bf16[1,2,128,128]{3,2,1,0:T(8,128)(2,1)S(1)}, u32[]{:S(2)}, u32[]{:S(2)}) collective-permute-start(bf16[1,2,128,128]{3,2,1,0:T(8,128)(2,1)S(1)} %get-tuple-element.27), channel_id=1, source_target_pairs={{1,0},{2,1},{3,2},{4,3},{5,4},{6,5},{7,6},{9,8},{10,9},{11,10},{12... | collective-permute-start | bytes 196616 | tf_op jit(solution)/shard_map/ppermute | solution.py:186
  57.6 6.2 %collective-permute-start.9 = (bf16[1,2,128,128]{3,2,1,0:T(8,128)(2,1)S(1)}, bf16[1,2,128,128]{3,2,1,0:T(8,128)(2,1)S(1)}, u32[]{:S(2)}, u32[]{:S(2)}) collective-permute-start(bf16[1,2,128,128]{3,2,1,0:T(8,128)(2,1)S(1)} %get-tuple-element.28), channel_id=1, source_target_pairs={{2,0},{3,1},{4,2},{5,3},{6,4},{7,5},{10,8},{11,9},{12,10},{13,11},... | collective-permute-start | bytes 196616 | tf_op jit(solution)/shard_map/ppermute | solution.py:186

commit v5 on v4

--- a/solution.py
+++ b/solution.py
@@ -40,13 +40,13 @@
     return jnp.concatenate(parts, axis=0)
 
 
-def attend(chunks, given, held, lens_ref, where_ref, q_ref, g_ref, *refs):
+def attend(chunks, given, held, lens_ref, q_ref, g_ref, *refs):
     refs = refs[given:]
     kv_refs = refs[:chunks]
     att_ref, dq_ref = refs[chunks : chunks + 2]
     part_refs = refs[chunks + 2 : 2 * chunks + 2]
     (bias_ref,) = refs[2 * chunks + 2 :]
-    run = where_ref[0]
+    run = lens_ref[SEGS]
     head, (skip, width) = pl.program_id(0), held
 
     def at(block, cols=slice(0, HD)):
@@ -152,7 +152,7 @@
     )(*parts, *before)
 
 
-def attend_heads(first, count, held, lens, run, wide_args, got, before):
+def attend_heads(first, count, held, facts, wide_args, got, before):
     chunks = len(got)
     vmem = pl.BlockSpec(memory_space=pltpu.VMEM)
     wide = pl.BlockSpec((ROWS, GROUP * HD), lambda h, *_: (0, first + h))
@@ -161,7 +161,7 @@
     return pl.pallas_call(
         functools.partial(attend, chunks, len(before), held),
         grid_spec=pltpu.PrefetchScalarGridSpec(
-            num_scalar_prefetch=2,
+            num_scalar_prefetch=1,
             grid=(count,),
             in_specs=[wide, wide]
             + [pl.BlockSpec(memory_space=pl.ANY)] * len(before)
@@ -170,7 +170,7 @@
             scratch_shapes=[pltpu.VMEM((ROWS, chunks * ROWS), jnp.float32)],
         ),
         out_shape=[big, big] + [part_shape] * chunks,
-        input_output_aliases={4 + i: i for i in range(len(before))},
+        input_output_aliases={3 + i: i for i in range(len(before))},
         cost_estimate=pl.CostEstimate(
             flops=12 * count * GROUP * ROWS * HD * chunks * ROWS,
             bytes_accessed=4 * count * GROUP * ROWS * HD * 2,
@@ -178,7 +178,7 @@
         ),
         compiler_params=pltpu.CompilerParams(vmem_limit_bytes=VMEM_LIMIT),
         name="attend",
-    )(lens, run, *wide_args, *before, *got)
+    )(facts, *wide_args, *before, *got)
 
 
 def shift(x, by, n):
@@ -191,6 +191,7 @@
     back = min(n - 1, -(-(MOST - 1) // ROWS))
     chunks = back + 1
     run = lax.axis_index("seq").astype(jnp.int32)[None]
+    facts = jnp.concatenate([lengths[0], run])
     got = []
     for first, count in PIECES:
         cols = slice(first * HD, (first + count) * HD)
@@ -200,7 +201,7 @@
     before, sums = (), ()
     for (first, count), runs in zip(PIECES, got):
         att, dq, *own = attend_heads(
-            first, count, (0, count), lengths[0], run, (queries, out_grad), runs, before
+            first, count, (0, count), facts, (queries, out_grad), runs, before
         )
         before = att, dq
         sent = [shift(own[c], -c, n) for c in range(1, chunks)]

time: 65.2 us -> 64.2 us (0.985)
  the two profiles are of different devices: /device:TPU:380 before, /device:TPU:284 now
where the time goes in v5:
time: 64.2 us; the launch traced here: 63.5 us
  starting transfers between devices  33 us (51%)
  Pallas kernels  16.4 us (26%)
  waiting for transfers between devices  10.8 us (17%)
  local copies, waits for them, and re-layouts  2.35 us (4%)
  between operations  0.87 us (1%)
    ppermute x16, starting transfers between devices, shift(): return lax.ppermute(x, 'seq', pairs)  33 us
    pallas_call x2, Pallas kernels, attend_heads(): pl.pallas_call(functools.partial(attend, chunks, len(before), held), grid...  14.8 us
    ppermute x16, waiting for transfers between devices, shift(): return lax.ppermute(x, 'seq', pairs)  10.8 us
    slice x8, local copies, waits for them, and re-layouts, shards(): both = jnp.concatenate([keys[:, cols], values[:, cols]], axis=1)  1.7 us
    pallas_call x2, Pallas kernels, total_heads(): pl.pallas_call(functools.partial(total, len(parts)), grid=(1,), in_specs=...  1.61 us
  transfers between devices with their start and end apart: 16, of which 5 were waited for; matrix products, arithmetic and copies ran while one was open for 0% of the time, Pallas kernels for 25%

profile of v5, /device:TPU:284, one launch (start us, length us, event | category | flops | bytes accessed | tf_op | source)
XLA Modules:
  0.0 63.5 jit_solution(6957015495133729005)
XLA Ops:
  0.6 0.0 slice-start
  0.6 0.0 slice-start.2
  0.7 0.9 %slice-done = bf16[128,384]{1,0:T(8,128)(2,1)S(1)} async-done(((bf16[128,512]{1,0:T(8,128)(2,1)}), bf16[128,384]{1,0:T(8,128)(2,1)S(1)}, s32[]{:S(2)}) %slice-start) | async-done | bytes 98328 | tf_op jit(solution)/shard_map/slice | solution.py:198
  1.5 0.0 slice-done.2
  1.6 3.3 %collective-permute-start = (bf16[128,768]{1,0:T(8,128)(2,1)S(1)}, bf16[128,768]{1,0:T(8,128)(2,1)S(1)}, u32[]{:S(2)}, u32[]{:S(2)}) collective-permute-start(bf16[128,768]{1,0:T(8,128)(2,1)S(1)} %pad_maximum_fusion.refs_0_), channel_id=1, source_target_pairs={{0,1},{1,2},{2,3},{3,4},{4,5},{5,6},{6,7},{8,9},{9,10},{10,11},{11... | collective-permute-start | bytes 589832 | tf_op jit(solution)/shard_map/ppermute | solution.py:186
  4.9 1.9 %collective-permute-start.1 = (bf16[128,768]{1,0:T(8,128)(2,1)S(1)}, bf16[128,768]{1,0:T(8,128)(2,1)S(1)}, u32[]{:S(2)}, u32[]{:S(2)}) collective-permute-start(bf16[128,768]{1,0:T(8,128)(2,1)S(1)} %pad_maximum_fusion.refs_0_), channel_id=1, source_target_pairs={{0,2},{1,3},{2,4},{3,5},{4,6},{5,7},{8,10},{9,11},{10,12},{11,13},... | collective-permute-start | bytes 589832 | tf_op jit(solution)/shard_map/ppermute | solution.py:186
  6.8 1.3 %collective-permute-start.2 = (bf16[128,768]{1,0:T(8,128)(2,1)S(1)}, bf16[128,768]{1,0:T(8,128)(2,1)S(1)}, u32[]{:S(2)}, u32[]{:S(2)}) collective-permute-start(bf16[128,768]{1,0:T(8,128)(2,1)S(1)} %pad_maximum_fusion.refs_0_), channel_id=1, source_target_pairs={{0,3},{1,4},{2,5},{3,6},{4,7},{8,11},{9,12},{10,13},{11,14},{12,15... | collective-permute-start | bytes 589832 | tf_op jit(solution)/shard_map/ppermute | solution.py:186
  8.1 1.3 %collective-permute-start.3 = (bf16[128,768]{1,0:T(8,128)(2,1)S(1)}, bf16[128,768]{1,0:T(8,128)(2,1)S(1)}, u32[]{:S(2)}, u32[]{:S(2)}) collective-permute-start(bf16[128,768]{1,0:T(8,128)(2,1)S(1)} %pad_maximum_fusion.refs_0_), channel_id=1, source_target_pairs={{0,4},{1,5},{2,6},{3,7},{8,12},{9,13},{10,14},{11,15},{16,20},{17,... | collective-permute-start | bytes 589832 | tf_op jit(solution)/shard_map/ppermute | solution.py:186
  9.4 0.0 slice-start.1
  9.4 0.0 slice-start.3
  9.4 0.7 %slice-done.1 = bf16[128,128]{1,0:T(8,128)(2,1)S(1)} async-done(((bf16[128,512]{1,0:T(8,128)(2,1)}), bf16[128,128]{1,0:T(8,128)(2,1)S(1)}, s32[]{:S(2)}) %slice-start.1) | async-done | bytes 32792 | tf_op jit(solution)/shard_map/slice | solution.py:198
  10.2 0.0 slice-done.3
  10.2 2.6 %collective-permute-start.4 = (bf16[128,256]{1,0:T(8,128)(2,1)S(1)}, bf16[128,256]{1,0:T(8,128)(2,1)S(1)}, u32[]{:S(2)}, u32[]{:S(2)}) collective-permute-start(bf16[128,256]{1,0:T(8,128)(2,1)S(1)} %pad_maximum_fusion.1.refs_2_), channel_id=1, source_target_pairs={{0,1},{1,2},{2,3},{3,4},{4,5},{5,6},{6,7},{8,9},{9,10},{10,11},{11... | collective-permute-start | bytes 196616 | tf_op jit(solution)/shard_map/ppermute | solution.py:186
  12.8 0.0 copy-start.1
  12.8 0.6 %copy-done.1 = s32[1,16]{1,0:T(1,128)S(1)} copy-done((s32[1,16]{1,0:T(1,128)S(1)}, s32[1,16]{1,0:T(1,128)}, u32[]{:S(2)}) %copy-start.1) | copy-done | bytes 88
  13.4 0.1 pad_add_fusion.lens_ref
  13.5 0.0 collective-permute-done.refs_1_
  13.5 2.0 %collective-permute-start.5 = (bf16[128,256]{1,0:T(8,128)(2,1)S(1)}, bf16[128,256]{1,0:T(8,128)(2,1)S(1)}, u32[]{:S(2)}, u32[]{:S(2)}) collective-permute-start(bf16[128,256]{1,0:T(8,128)(2,1)S(1)} %pad_maximum_fusion.1.refs_2_), channel_id=1, source_target_pairs={{0,2},{1,3},{2,4},{3,5},{4,6},{5,7},{8,10},{9,11},{10,12},{11,13},... | collective-permute-start | bytes 196616 | tf_op jit(solution)/shard_map/ppermute | solution.py:186
  15.6 0.0 collective-permute-done.1.refs_2_
  15.6 1.3 %collective-permute-start.6 = (bf16[128,256]{1,0:T(8,128)(2,1)S(1)}, bf16[128,256]{1,0:T(8,128)(2,1)S(1)}, u32[]{:S(2)}, u32[]{:S(2)}) collective-permute-start(bf16[128,256]{1,0:T(8,128)(2,1)S(1)} %pad_maximum_fusion.1.refs_2_), channel_id=1, source_target_pairs={{0,3},{1,4},{2,5},{3,6},{4,7},{8,11},{9,12},{10,13},{11,14},{12,15... | collective-permute-start | bytes 196616 | tf_op jit(solution)/shard_map/ppermute | solution.py:186
  16.9 2.0 %collective-permute-done.2.refs_3_ = bf16[128,768]{1,0:T(8,128)(2,1)S(1)} collective-permute-done((bf16[128,768]{1,0:T(8,128)(2,1)S(1)}, bf16[128,768]{1,0:T(8,128)(2,1)S(1)}, u32[]{:S(2)}, u32[]{:S(2)}) %collective-permute-start.2) | collective-permute-done | bytes 196640 | tf_op jit(solution)/shard_map/ppermute | solution.py:186
  18.9 5.2 %collective-permute-done.3.refs_4_ = bf16[128,768]{1,0:T(8,128)(2,1)S(1)} collective-permute-done((bf16[128,768]{1,0:T(8,128)(2,1)S(1)}, bf16[128,768]{1,0:T(8,128)(2,1)S(1)}, u32[]{:S(2)}, u32[]{:S(2)}) %collective-permute-start.3) | collective-permute-done | bytes 196640 | tf_op jit(solution)/shard_map/ppermute | solution.py:186
  24.0 9.8 %attend.2 = (bf16[128,4096]{1,0:T(8,128)(2,1)}, bf16[128,4096]{1,0:T(8,128)(2,1)}, bf16[3,2,128,128]{3,2,1,0:T(8,128)(2,1)S(1)}, bf16[3,2,128,128]{3,2,1,0:T(8,1...) custom-call(s32[17]{0:T(128)S(1)} %pad_add_fusion.lens_ref, ...), custom_call_target="tpu_custom_call" | custom-call | flops 3019898880 | bytes 3145728 | tf_op jit(solution)/shard_map/attend/pallas_call | solution.py:161
  33.9 1.9 %collective-permute-start.12 = (bf16[3,2,128,128]{3,2,1,0:T(8,128)(2,1)S(1)}, bf16[3,2,128,128]{3,2,1,0:T(8,128)(2,1)S(1)}, u32[]{:S(2)}, u32[]{:S(2)}) collective-permute-start(bf16[3,2,128,128]{3,2,1,0:T(8,128)(2,1)S(1)} %get-tuple-element.32), channel_id=1, source_target_pairs={{1,0},{2,1},{3,2},{4,3},{5,4},{6,5},{7,6},{9,8},{10,9},{11,10},{12... | collective-permute-start | bytes 589832 | tf_op jit(solution)/shard_map/ppermute | solution.py:186
  35.8 1.9 %collective-permute-start.13 = (bf16[3,2,128,128]{3,2,1,0:T(8,128)(2,1)S(1)}, bf16[3,2,128,128]{3,2,1,0:T(8,128)(2,1)S(1)}, u32[]{:S(2)}, u32[]{:S(2)}) collective-permute-start(bf16[3,2,128,128]{3,2,1,0:T(8,128)(2,1)S(1)} %get-tuple-element.33), channel_id=1, source_target_pairs={{2,0},{3,1},{4,2},{5,3},{6,4},{7,5},{10,8},{11,9},{12,10},{13,11},... | collective-permute-start | bytes 589832 | tf_op jit(solution)/shard_map/ppermute | solution.py:186
  37.7 0.0 collective-permute-done.4.refs_3_
  37.7 1.3 %collective-permute-start.14 = (bf16[3,2,128,128]{3,2,1,0:T(8,128)(2,1)S(1)}, bf16[3,2,128,128]{3,2,1,0:T(8,128)(2,1)S(1)}, u32[]{:S(2)}, u32[]{:S(2)}) collective-permute-start(bf16[3,2,128,128]{3,2,1,0:T(8,128)(2,1)S(1)} %get-tuple-element.34), channel_id=1, source_target_pairs={{3,0},{4,1},{5,2},{6,3},{7,4},{11,8},{12,9},{13,10},{14,11},{15,12... | collective-permute-start | bytes 589832 | tf_op jit(solution)/shard_map/ppermute | solution.py:186
  39.0 0.0 collective-permute-done.5.refs_4_
  39.1 1.3 %collective-permute-start.7 = (bf16[128,256]{1,0:T(8,128)(2,1)S(1)}, bf16[128,256]{1,0:T(8,128)(2,1)S(1)}, u32[]{:S(2)}, u32[]{:S(2)}) collective-permute-start(bf16[128,256]{1,0:T(8,128)(2,1)S(1)} %pad_maximum_fusion.1.refs_2_), channel_id=1, source_target_pairs={{0,4},{1,5},{2,6},{3,7},{8,12},{9,13},{10,14},{11,15},{16,20},{17,... | collective-permute-start | bytes 196616 | tf_op jit(solution)/shard_map/ppermute | solution.py:186
  40.4 0.0 collective-permute-done.6.refs_5_
  40.4 6.1 %collective-permute-start.15 = (bf16[3,2,128,128]{3,2,1,0:T(8,128)(2,1)S(1)}, bf16[3,2,128,128]{3,2,1,0:T(8,128)(2,1)S(1)}, u32[]{:S(2)}, u32[]{:S(2)}) collective-permute-start(bf16[3,2,128,128]{3,2,1,0:T(8,128)(2,1)S(1)} %get-tuple-element.35), channel_id=1, source_target_pairs={{4,0},{5,1},{6,2},{7,3},{12,8},{13,9},{14,10},{15,11},{20,16},{21,... | collective-permute-start | bytes 589832 | tf_op jit(solution)/shard_map/ppermute | solution.py:186
  46.4 0.3 collective-permute-done.7.refs_6_
  46.7 0.0 copy-done
  46.7 4.9 %attend.3 = (bf16[128,4096]{1,0:T(8,128)(2,1)}, bf16[128,4096]{1,0:T(8,128)(2,1)}, bf16[1,2,128,128]{3,2,1,0:T(8,128)(2,1)S(1)}, bf16[1,2,128,128]{3,2,1,0:T(8,1...) custom-call(s32[17]{0:T(128)S(1)} %pad_add_fusion.lens_ref, ...), custom_call_target="tpu_custom_call", output_to_operand_aliasing={{0}: (3, {}), {1}: (4, {})} | custom-call | flops 1006632960 | bytes 1048576 | tf_op jit(solution)/shard_map/attend/pallas_call | solution.py:161
  51.7 1.3 %collective-permute-start.10 = (bf16[1,2,128,128]{3,2,1,0:T(8,128)(2,1)S(1)}, bf16[1,2,128,128]{3,2,1,0:T(8,128)(2,1)S(1)}, u32[]{:S(2)}, u32[]{:S(2)}) collective-permute-start(bf16[1,2,128,128]{3,2,1,0:T(8,128)(2,1)S(1)} %get-tuple-element.29), channel_id=1, source_target_pairs={{3,0},{4,1},{5,2},{6,3},{7,4},{11,8},{12,9},{13,10},{14,11},{15,12... | collective-permute-start | bytes 196616 | tf_op jit(solution)/shard_map/ppermute | solution.py:186
  53.0 0.0 collective-permute-done.12.refs_1_
  53.0 1.3 %collective-permute-start.11 = (bf16[1,2,128,128]{3,2,1,0:T(8,128)(2,1)S(1)}, bf16[1,2,128,128]{3,2,1,0:T(8,128)(2,1)S(1)}, u32[]{:S(2)}, u32[]{:S(2)}) collective-permute-start(bf16[1,2,128,128]{3,2,1,0:T(8,128)(2,1)S(1)} %get-tuple-element.30), channel_id=1, source_target_pairs={{4,0},{5,1},{6,2},{7,3},{12,8},{13,9},{14,10},{15,11},{20,16},{21,... | collective-permute-start | bytes 196616 | tf_op jit(solution)/shard_map/ppermute | solution.py:186
  54.3 0.0 collective-permute-done.13.refs_2_
  54.3 2.3 %collective-permute-start.8 = (bf16[1,2,128,128]{3,2,1,0:T(8,128)(2,1)S(1)}, bf16[1,2,128,128]{3,2,1,0:T(8,128)(2,1)S(1)}, u32[]{:S(2)}, u32[]{:S(2)}) collective-permute-start(bf16[1,2,128,128]{3,2,1,0:T(8,128)(2,1)S(1)} %get-tuple-element.27), channel_id=1, source_target_pairs={{1,0},{2,1},{3,2},{4,3},{5,4},{6,5},{7,6},{9,8},{10,9},{11,10},{12... | collective-permute-start | bytes 196616 | tf_op jit(solution)/shard_map/ppermute | solution.py:186
  56.6 0.0 collective-permute-done.14.refs_3_
  56.6 1.9 %collective-permute-start.9 = (bf16[1,2,128,128]{3,2,1,0:T(8,128)(2,1)S(1)}, bf16[1,2,128,128]{3,2,1,0:T(8,128)(2,1)S(1)}, u32[]{:S(2)}, u32[]{:S(2)}) collective-permute-start(bf16[1,2,128,128]{3,2,1,0:T(8,128)(2,1)S(1)} %get-tuple-element.28), channel_id=1, source_target_pairs={{2,0},{3,1},{4,2},{5,3},{6,4},{7,5},{10,8},{11,9},{12,10},{13,11},... | collective-permute-start | bytes 196616 | tf_op jit(solution)/shard_map/ppermute | solution.py:186
  58.5 0.0 collective-permute-done.15.refs_4_
  58.6 0.9 %total.2 = (bf16[128,512]{1,0:T(8,128)(2,1)}, bf16[128,512]{1,0:T(8,128)(2,1)}) custom-call(bf16[3,2,128,128]{3,2,1,0:T(8,128)(2,1)S(1)} %get-tuple-element.31.refs_0_, bf16[3,2,128,128]{3,2,1,0:T(8,128)(2,1)S(1)} %collective-permute-done.12.refs_1_, bf16[3,2,128,128]{3,2,1,0:T(8,128)(2,1)S(1)} %collective-permute-done.13.refs_2_, ...), custom_call_target="tpu_custom_call" | custom-call | flops 491520 | bytes 1179648 | tf_op jit(solution)/shard_map/total/pallas_call | solution.py:137
  59.4 0.0 collective-permute-done.10.refs_3_
  59.4 0.0 collective-permute-done.11.refs_4_
  59.4 1.9 %collective-permute-done.8.refs_1_ = bf16[1,2,128,128]{3,2,1,0:T(8,128)(2,1)S(1)} collective-permute-done((bf16[1,2,128,128]{3,2,1,0:T(8,128)(2,1)S(1)}, bf16[1,2,128,128]{3,2,1,0:T(8,128)(2,1)S(1)}, u32[]{:S(2)}, u32[]{:S(2)}) %collective-permute-start.8) | collective-permute-done | bytes 65568 | tf_op jit(solution)/shard_map/ppermute | solution.py:186
  61.3 1.4 %collective-permute-done.9.refs_2_ = bf16[1,2,128,128]{3,2,1,0:T(8,128)(2,1)S(1)} collective-permute-done((bf16[1,2,128,128]{3,2,1,0:T(8,128)(2,1)S(1)}, bf16[1,2,128,128]{3,2,1,0:T(8,128)(2,1)S(1)}, u32[]{:S(2)}, u32[]{:S(2)}) %collective-permute-start.9) | collective-permute-done | bytes 65568 | tf_op jit(solution)/shard_map/ppermute | solution.py:186
  62.8 0.7 %total.3 = (bf16[128,512]{1,0:T(8,128)(2,1)}, bf16[128,512]{1,0:T(8,128)(2,1)}) custom-call(bf16[1,2,128,128]{3,2,1,0:T(8,128)(2,1)S(1)} %get-tuple-element.26.refs_0_, bf16[1,2,128,128]{3,2,1,0:T(8,128)(2,1)S(1)} %collective-permute-done.8.refs_1_, ...), custom_call_target="tpu_custom_call", output_to_operand_aliasing={{0}: (5, {}), {1}: (6, {})} | custom-call | flops 163840 | bytes 393216 | tf_op jit(solution)/shard_map/total/pallas_call | solution.py:137
  (3 shorter events, 0.0 us)
Async XLA Ops:
  0.6 0.9 %slice-start = ((bf16[128,512]{1,0:T(8,128)(2,1)}), bf16[128,384]{1,0:T(8,128)(2,1)S(1)}, s32[]{:S(2)}) async-start(bf16[128,512]{1,0:T(8,128)(2,1)} %param.6), calls=%async_computation | async-start | bytes 196608 | tf_op jit(solution)/shard_map/slice | solution.py:198
  0.6 0.9 %slice-start.2 = ((bf16[128,512]{1,0:T(8,128)(2,1)}), bf16[128,384]{1,0:T(8,128)(2,1)S(1)}, s32[]{:S(2)}) async-start(bf16[128,512]{1,0:T(8,128)(2,1)} %param.7), calls=%async_computation.2 | async-start | bytes 196608 | tf_op jit(solution)/shard_map/slice | solution.py:198
  1.6 11.9 %collective-permute-start = (bf16[128,768]{1,0:T(8,128)(2,1)S(1)}, bf16[128,768]{1,0:T(8,128)(2,1)S(1)}, u32[]{:S(2)}, u32[]{:S(2)}) collective-permute-start(bf16[128,768]{1,0:T(8,128)(2,1)S(1)} %pad_maximum_fusion.refs_0_), channel_id=1, source_target_pairs={{0,1},{1,2},{2,3},{3,4},{4,5},{5,6},{6,7},{8,9},{9,10},{10,11},{11... | collective-permute-start | bytes 589832 | tf_op jit(solution)/shard_map/ppermute | solution.py:186
  4.9 10.7 %collective-permute-start.1 = (bf16[128,768]{1,0:T(8,128)(2,1)S(1)}, bf16[128,768]{1,0:T(8,128)(2,1)S(1)}, u32[]{:S(2)}, u32[]{:S(2)}) collective-permute-start(bf16[128,768]{1,0:T(8,128)(2,1)S(1)} %pad_maximum_fusion.refs_0_), channel_id=1, source_target_pairs={{0,2},{1,3},{2,4},{3,5},{4,6},{5,7},{8,10},{9,11},{10,12},{11,13},... | collective-permute-start | bytes 589832 | tf_op jit(solution)/shard_map/ppermute | solution.py:186
  6.8 12.1 %collective-permute-start.2 = (bf16[128,768]{1,0:T(8,128)(2,1)S(1)}, bf16[128,768]{1,0:T(8,128)(2,1)S(1)}, u32[]{:S(2)}, u32[]{:S(2)}) collective-permute-start(bf16[128,768]{1,0:T(8,128)(2,1)S(1)} %pad_maximum_fusion.refs_0_), channel_id=1, source_target_pairs={{0,3},{1,4},{2,5},{3,6},{4,7},{8,11},{9,12},{10,13},{11,14},{12,15... | collective-permute-start | bytes 589832 | tf_op jit(solution)/shard_map/ppermute | solution.py:186
  8.1 15.9 %collective-permute-start.3 = (bf16[128,768]{1,0:T(8,128)(2,1)S(1)}, bf16[128,768]{1,0:T(8,128)(2,1)S(1)}, u32[]{:S(2)}, u32[]{:S(2)}) collective-permute-start(bf16[128,768]{1,0:T(8,128)(2,1)S(1)} %pad_maximum_fusion.refs_0_), channel_id=1, source_target_pairs={{0,4},{1,5},{2,6},{3,7},{8,12},{9,13},{10,14},{11,15},{16,20},{17,... | collective-permute-start | bytes 589832 | tf_op jit(solution)/shard_map/ppermute | solution.py:186
  9.4 0.8 %slice-start.1 = ((bf16[128,512]{1,0:T(8,128)(2,1)}), bf16[128,128]{1,0:T(8,128)(2,1)S(1)}, s32[]{:S(2)}) async-start(bf16[128,512]{1,0:T(8,128)(2,1)} %param.6), calls=%async_computation.1 | async-start | bytes 65536 | tf_op jit(solution)/shard_map/slice | solution.py:198
  9.4 0.8 %slice-start.3 = ((bf16[128,512]{1,0:T(8,128)(2,1)}), bf16[128,128]{1,0:T(8,128)(2,1)S(1)}, s32[]{:S(2)}) async-start(bf16[128,512]{1,0:T(8,128)(2,1)} %param.7), calls=%async_computation.3 | async-start | bytes 65536 | tf_op jit(solution)/shard_map/slice | solution.py:198
  10.2 27.5 %collective-permute-start.4 = (bf16[128,256]{1,0:T(8,128)(2,1)S(1)}, bf16[128,256]{1,0:T(8,128)(2,1)S(1)}, u32[]{:S(2)}, u32[]{:S(2)}) collective-permute-start(bf16[128,256]{1,0:T(8,128)(2,1)S(1)} %pad_maximum_fusion.1.refs_2_), channel_id=1, source_target_pairs={{0,1},{1,2},{2,3},{3,4},{4,5},{5,6},{6,7},{8,9},{9,10},{10,11},{11... | collective-permute-start | bytes 196616 | tf_op jit(solution)/shard_map/ppermute | solution.py:186
  12.8 0.7 %copy-start.1 = (s32[1,16]{1,0:T(1,128)S(1)}, s32[1,16]{1,0:T(1,128)}, u32[]{:S(2)}) copy-start(s32[1,16]{1,0:T(1,128)} %param.8) | copy-start | bytes 196
  13.5 33.2 %copy-start = (bf16[128,4096]{1,0:T(8,128)(2,1)S(1)}, bf16[128,4096]{1,0:T(8,128)(2,1)}, u32[]{:S(2)}) copy-start(bf16[128,4096]{1,0:T(8,128)(2,1)} %q_ref.3) | copy-start | bytes 3145732
  13.5 25.5 %collective-permute-start.5 = (bf16[128,256]{1,0:T(8,128)(2,1)S(1)}, bf16[128,256]{1,0:T(8,128)(2,1)S(1)}, u32[]{:S(2)}, u32[]{:S(2)}) collective-permute-start(bf16[128,256]{1,0:T(8,128)(2,1)S(1)} %pad_maximum_fusion.1.refs_2_), channel_id=1, source_target_pairs={{0,2},{1,3},{2,4},{3,5},{4,6},{5,7},{8,10},{9,11},{10,12},{11,13},... | collective-permute-start | bytes 196616 | tf_op jit(solution)/shard_map/ppermute | solution.py:186
  15.6 24.7 %collective-permute-start.6 = (bf16[128,256]{1,0:T(8,128)(2,1)S(1)}, bf16[128,256]{1,0:T(8,128)(2,1)S(1)}, u32[]{:S(2)}, u32[]{:S(2)}) collective-permute-start(bf16[128,256]{1,0:T(8,128)(2,1)S(1)} %pad_maximum_fusion.1.refs_2_), channel_id=1, source_target_pairs={{0,3},{1,4},{2,5},{3,6},{4,7},{8,11},{9,12},{10,13},{11,14},{12,15... | collective-permute-start | bytes 196616 | tf_op jit(solution)/shard_map/ppermute | solution.py:186
  33.9 19.1 %collective-permute-start.12 = (bf16[3,2,128,128]{3,2,1,0:T(8,128)(2,1)S(1)}, bf16[3,2,128,128]{3,2,1,0:T(8,128)(2,1)S(1)}, u32[]{:S(2)}, u32[]{:S(2)}) collective-permute-start(bf16[3,2,128,128]{3,2,1,0:T(8,128)(2,1)S(1)} %get-tuple-element.32), channel_id=1, source_target_pairs={{1,0},{2,1},{3,2},{4,3},{5,4},{6,5},{7,6},{9,8},{10,9},{11,10},{12... | collective-permute-start | bytes 589832 | tf_op jit(solution)/shard_map/ppermute | solution.py:186
  35.8 18.5 %collective-permute-start.13 = (bf16[3,2,128,128]{3,2,1,0:T(8,128)(2,1)S(1)}, bf16[3,2,128,128]{3,2,1,0:T(8,128)(2,1)S(1)}, u32[]{:S(2)}, u32[]{:S(2)}) collective-permute-start(bf16[3,2,128,128]{3,2,1,0:T(8,128)(2,1)S(1)} %get-tuple-element.33), channel_id=1, source_target_pairs={{2,0},{3,1},{4,2},{5,3},{6,4},{7,5},{10,8},{11,9},{12,10},{13,11},... | collective-permute-start | bytes 589832 | tf_op jit(solution)/shard_map/ppermute | solution.py:186
  37.7 18.9 %collective-permute-start.14 = (bf16[3,2,128,128]{3,2,1,0:T(8,128)(2,1)S(1)}, bf16[3,2,128,128]{3,2,1,0:T(8,128)(2,1)S(1)}, u32[]{:S(2)}, u32[]{:S(2)}) collective-permute-start(bf16[3,2,128,128]{3,2,1,0:T(8,128)(2,1)S(1)} %get-tuple-element.34), channel_id=1, source_target_pairs={{3,0},{4,1},{5,2},{6,3},{7,4},{11,8},{12,9},{13,10},{14,11},{15,12... | collective-permute-start | bytes 589832 | tf_op jit(solution)/shard_map/ppermute | solution.py:186
  39.1 7.7 %collective-permute-start.7 = (bf16[128,256]{1,0:T(8,128)(2,1)S(1)}, bf16[128,256]{1,0:T(8,128)(2,1)S(1)}, u32[]{:S(2)}, u32[]{:S(2)}) collective-permute-start(bf16[128,256]{1,0:T(8,128)(2,1)S(1)} %pad_maximum_fusion.1.refs_2_), channel_id=1, source_target_pairs={{0,4},{1,5},{2,6},{3,7},{8,12},{9,13},{10,14},{11,15},{16,20},{17,... | collective-permute-start | bytes 196616 | tf_op jit(solution)/shard_map/ppermute | solution.py:186
  40.4 18.2 %collective-permute-start.15 = (bf16[3,2,128,128]{3,2,1,0:T(8,128)(2,1)S(1)}, bf16[3,2,128,128]{3,2,1,0:T(8,128)(2,1)S(1)}, u32[]{:S(2)}, u32[]{:S(2)}) collective-permute-start(bf16[3,2,128,128]{3,2,1,0:T(8,128)(2,1)S(1)} %get-tuple-element.35), channel_id=1, source_target_pairs={{4,0},{5,1},{6,2},{7,3},{12,8},{13,9},{14,10},{15,11},{20,16},{21,... | collective-permute-start | bytes 589832 | tf_op jit(solution)/shard_map/ppermute | solution.py:186
  51.7 7.8 %collective-permute-start.10 = (bf16[1,2,128,128]{3,2,1,0:T(8,128)(2,1)S(1)}, bf16[1,2,128,128]{3,2,1,0:T(8,128)(2,1)S(1)}, u32[]{:S(2)}, u32[]{:S(2)}) collective-permute-start(bf16[1,2,128,128]{3,2,1,0:T(8,128)(2,1)S(1)} %get-tuple-element.29), channel_id=1, source_target_pairs={{3,0},{4,1},{5,2},{6,3},{7,4},{11,8},{12,9},{13,10},{14,11},{15,12... | collective-permute-start | bytes 196616 | tf_op jit(solution)/shard_map/ppermute | solution.py:186
  53.0 6.5 %collective-permute-start.11 = (bf16[1,2,128,128]{3,2,1,0:T(8,128)(2,1)S(1)}, bf16[1,2,128,128]{3,2,1,0:T(8,128)(2,1)S(1)}, u32[]{:S(2)}, u32[]{:S(2)}) collective-permute-start(bf16[1,2,128,128]{3,2,1,0:T(8,128)(2,1)S(1)} %get-tuple-element.30), channel_id=1, source_target_pairs={{4,0},{5,1},{6,2},{7,3},{12,8},{13,9},{14,10},{15,11},{20,16},{21,... | collective-permute-start | bytes 196616 | tf_op jit(solution)/shard_map/ppermute | solution.py:186
  54.3 7.1 %collective-permute-start.8 = (bf16[1,2,128,128]{3,2,1,0:T(8,128)(2,1)S(1)}, bf16[1,2,128,128]{3,2,1,0:T(8,128)(2,1)S(1)}, u32[]{:S(2)}, u32[]{:S(2)}) collective-permute-start(bf16[1,2,128,128]{3,2,1,0:T(8,128)(2,1)S(1)} %get-tuple-element.27), channel_id=1, source_target_pairs={{1,0},{2,1},{3,2},{4,3},{5,4},{6,5},{7,6},{9,8},{10,9},{11,10},{12... | collective-permute-start | bytes 196616 | tf_op jit(solution)/shard_map/ppermute | solution.py:186
  56.6 6.2 %collective-permute-start.9 = (bf16[1,2,128,128]{3,2,1,0:T(8,128)(2,1)S(1)}, bf16[1,2,128,128]{3,2,1,0:T(8,128)(2,1)S(1)}, u32[]{:S(2)}, u32[]{:S(2)}) collective-permute-start(bf16[1,2,128,128]{3,2,1,0:T(8,128)(2,1)S(1)} %get-tuple-element.28), channel_id=1, source_target_pairs={{2,0},{3,1},{4,2},{5,3},{6,4},{7,5},{10,8},{11,9},{12,10},{13,11},... | collective-permute-start | bytes 196616 | tf_op jit(solution)/shard_map/ppermute | solution.py:186
